TPU v7x, 32 devices: a whole 2x2x4 slice. The times are simulated.
32 devices in a mesh: region: 2 (over y), tile: 4 (over z), member: 2 (over x), date: 2 (over core).
Axes of the slice: x: 2, y: 2, z: 4, core: 2. Of those that a mesh axis runs over, the one named last changes fastest.
Arguments:
- sim_lai: bfloat16 [2, 32, 4, 32, 512], P('date', ('region', 'tile'), 'member'), parts along dimension 1, may hold values from 0 to 6
- owner_ids: int32 [2, 32], P('date', ('region', 'tile')), parts along dimension 1, may hold values from 0 to 3, as said below
- cloud_words: int32 [2, 32, 32], P('date', ('region', 'tile')), parts along dimension 1, may hold values from -2147483648 to 2147483646
- scene_lai: bfloat16 [2, 8, 8, 16, 256], P('date', ('region', 'tile'), 'member'), parts along dimension 1, may hold values from 0 to 6
- scene_sigma: bfloat16 [2, 8, 8, 16, 256], P('date', ('region', 'tile'), 'member'), parts along dimension 1, may hold values from 1 to 4
- mtf_taps: float32 [2, 7], replicated, may hold values from 0.1 to 1
Outputs:
- lai_update: bfloat16 [2, 32, 4, 32, 512], P('date', ('region', 'tile'), 'member'), parts along dimension 1
There are 2 independent parts, one for each index of `region`. A program takes and returns all parts, laid end to end along the dimension named above; an argument that names none is the same for every part. Nothing has to cross between parts.
Inputs may be any that keep to these rules, and one draw needn't show every extreme that they name: `owner_ids`: on each date each device along tile, holding 4 consecutive tiles, sends either none or exactly 2 of them to each owner; some owner receives 2 tiles from every device.
All inputs are finite; a program needn't handle non-finite values.
Results may differ from a plain program's by a relative error of at most 0.013.
The roundings to bfloat16 on the way count: a program that leaves them out, or rounds other values in their place, can miss the bound.
Values may be sent and summed in bfloat16 or wider, within the bound.
No kernel may reach another device: no remote copies, remote signals or barrier semaphores. Data moves between devices by JAX's collectives and lax.ppermute only.
A program may use at most 64 MiB of HBM per device.

v0:
```python
import jax
import jax.numpy as jnp
from jax import lax
from jax.sharding import PartitionSpec as P

CAP = 2


def band_tables(mtf_taps, tile_rows, tile_cols):
    kernel = mtf_taps / jnp.sum(mtf_taps, axis=1, keepdims=True)
    half_rows = tile_rows // 2
    half_cols = tile_cols // 2
    tap_reach = mtf_taps.shape[1] // 2
    out_rows = lax.broadcasted_iota(jnp.int32, (half_rows, tile_rows), 0)
    in_rows = lax.broadcasted_iota(jnp.int32, (half_rows, tile_rows), 1)
    in_cols = lax.broadcasted_iota(jnp.int32, (tile_cols, half_cols), 0)
    out_cols = lax.broadcasted_iota(jnp.int32, (tile_cols, half_cols), 1)
    row_table = jnp.zeros((half_rows, tile_rows), jnp.float32)
    col_table = jnp.zeros((tile_cols, half_cols), jnp.float32)
    for offset in range(mtf_taps.shape[1]):
        row_table = row_table + jnp.where(
            in_rows == 2 * out_rows + offset - tap_reach, kernel[0, offset], 0.0
        )
        col_table = col_table + jnp.where(
            in_cols == 2 * out_cols + offset - tap_reach, kernel[1, offset], 0.0
        )
    return (row_table.astype(jnp.bfloat16), col_table.astype(jnp.bfloat16))


def cloud_weights(words, half_rows, half_cols):
    shifts = jnp.arange(32)
    bit_values = jnp.bitwise_and(jnp.right_shift(words[..., None], shifts), 1)
    cells = bit_values.reshape(words.shape[:-1] + (half_rows // 2, half_cols // 2)).astype(
        jnp.float32
    )
    return jnp.repeat(jnp.repeat(cells, 2, axis=-2), 2, axis=-1)


def weighted_misfit(valid, observed, sigma_obs, predicted):
    sigma_wide = sigma_obs.astype(jnp.float32)
    gap = observed.astype(jnp.float32) - predicted.astype(jnp.float32)
    return (valid * gap / (sigma_wide * sigma_wide)).astype(jnp.bfloat16)


def degrade(fields, row_table, col_table):
    blurred = jnp.einsum(
        "ir,...rc->...ic", row_table, fields, preferred_element_type=jnp.float32
    ).astype(jnp.bfloat16)
    return jnp.einsum(
        "...ic,cj->...ij", blurred, col_table, preferred_element_type=jnp.float32
    ).astype(jnp.bfloat16)


def adjoint_map(misfit, row_table, col_table):
    spread = jnp.einsum(
        "...ij,cj->...ic", misfit, col_table, preferred_element_type=jnp.float32
    ).astype(jnp.bfloat16)
    return jnp.einsum(
        "ir,...ic->...rc", row_table, spread, preferred_element_type=jnp.float32
    ).astype(jnp.bfloat16)


def per_device(sim_lai, owner_ids, cloud_words, scene_lai, scene_sigma, mtf_taps):
    tile_count = lax.axis_size("tile")
    tiles_here = sim_lai.shape[1]
    members_here = sim_lai.shape[2]
    tile_rows = sim_lai.shape[3]
    tile_cols = sim_lai.shape[4]
    half_rows = tile_rows // 2
    half_cols = tile_cols // 2
    slot_count = tile_count * CAP
    row_table, col_table = band_tables(mtf_taps, tile_rows, tile_cols)
    owners = owner_ids[0]
    same_owner = owners[:, None] == owners[None, :]
    earlier = lax.broadcasted_iota(jnp.int32, (tiles_here, tiles_here), 0) < lax.broadcasted_iota(
        jnp.int32, (tiles_here, tiles_here), 1
    )
    rank = jnp.sum(jnp.logical_and(same_owner, earlier).astype(jnp.int32), axis=0)
    target = owners * CAP + rank
    slot_onehot = lax.broadcasted_iota(jnp.int32, (slot_count, tiles_here), 0) == target[None, :]
    onehot_bf = slot_onehot.astype(jnp.bfloat16)
    scenes, sigmas = (
        lax.all_gather(scene_lai, "member", axis=2, tiled=True),
        lax.all_gather(scene_sigma, "member", axis=2, tiled=True),
    )
    local_tiles = sim_lai[0]
    words_out = jnp.sum(jnp.where(slot_onehot[:, :, None], cloud_words[0][None, :, :], 0), axis=1)
    words_out = words_out.reshape(tile_count, CAP, -1)
    scenes = scenes.reshape(slot_count, 1, half_rows, half_cols)
    sigmas = sigmas.reshape(slot_count, 1, half_rows, half_cols)
    flat = local_tiles.reshape(tiles_here, -1)
    outgoing = (
        jnp.dot(onehot_bf, flat, preferred_element_type=jnp.float32)
        .astype(jnp.bfloat16)
        .reshape(tile_count, CAP, members_here, tile_rows, tile_cols)
    )
    arrived, arrived_words = (
        lax.all_to_all(outgoing, "tile", split_axis=0, concat_axis=0, tiled=True),
        lax.all_to_all(words_out, "tile", split_axis=0, concat_axis=0, tiled=True),
    )
    arrived = arrived.reshape(slot_count, members_here, tile_rows, tile_cols)
    valid = cloud_weights(arrived_words.reshape(slot_count, -1), half_rows, half_cols)[:, None]
    misfit = weighted_misfit(valid, scenes, sigmas, degrade(arrived, row_table, col_table))
    answered = adjoint_map(misfit, row_table, col_table).reshape(
        tile_count, CAP, members_here, tile_rows, tile_cols
    )
    returned = lax.all_to_all(answered, "tile", split_axis=0, concat_axis=0, tiled=True)
    flat = returned.reshape(slot_count, -1)
    lai_update = (
        jnp.dot(onehot_bf.T, flat, preferred_element_type=jnp.float32)
        .astype(jnp.bfloat16)
        .reshape(tiles_here, members_here, tile_rows, tile_cols)
    )
    return lai_update[None]


def solution(mesh):
    placed = (
        P("date", ("region", "tile"), "member", None, None),
        P("date", ("region", "tile")),
        P("date", ("region", "tile"), None),
        P("date", ("region", "tile"), "member", None, None),
        P("date", ("region", "tile"), "member", None, None),
        P(),
    )
    return jax.shard_map(
        per_device,
        mesh=mesh,
        in_specs=placed,
        out_specs=P("date", ("region", "tile"), "member", None, None),
        check_vma=False,
    )
```

profile of v0, /device:TPU:0, one launch (start us, length us, event | category | flops | bytes accessed | tf_op | source)
XLA Modules:
  0.0 74.5 jit_solution(14291288457161708068)
XLA Ops:
  0.0 0.7 copy-done.4
  0.7 0.1 convert_reduce_fusion
  0.8 0.1 iota_compare_fusion.15
  0.8 0.6 copy-done.3
  1.4 0.7 select_reduce_fusion
  2.1 6.3 %all-to-all-start = ((s32[4,2,32]{2,1,0:T(2,128)}), s32[4,2,32]{2,1,0:T(2,128)S(1)}, u32[]{:S(2)}, u32[]{:S(2)}) async-start(s32[4,2,32]{2,1,0:T(2,128)} %bitcast.4), calls=%async_computation | async-start | bytes 8192 | tf_op jit(solution)/shard_map/all_to_all | solution.py:99
  8.5 0.0 copy-start.2
  8.5 0.7 copy-done.2
  9.2 0.1 reduce_sum.32
  9.3 0.1 broadcast_divide_fusion
  9.3 0.7 fusion.27
  10.0 1.1 %reshape_squeeze.3 = bf16[4,32768]{1,0:T(4,128)(2,1)S(1)} reshape(bf16[1,4,2,32,512]{4,3,2,1,0:T(8,128)(2,1)} %param.6) | data formatting | bytes 524288 | tf_op jit(solution)/shard_map/reshape;squeeze | solution.py:91
  11.2 0.0 copy-start
  11.2 0.4 convolution_convert_fusion
  11.6 0.3 copy-done
  11.9 4.7 %all_gather.6 = bf16[1,1,8,16,256]{4,3,1,0,2:T(8,128)(2,1)S(1)} all-gather(bf16[1,1,4,16,256]{4,3,1,0,2:T(8,128)(2,1)S(1)} %bitcast.87), channel_id=1, replica_groups=mesh['region'=2,'tile'=4,'member'=2,'date'=2] {'member'}, dimensions={2}, use_global_device_ids=true | all-gather | bytes 98304 | tf_op jit(solution)/shard_map/all_gather | solution.py:83
  16.7 4.6 %all_gather.7 = bf16[1,1,8,16,256]{4,3,1,0,2:T(8,128)(2,1)S(1)} all-gather(bf16[1,1,4,16,256]{4,3,1,0,2:T(8,128)(2,1)S(1)} %bitcast.88), channel_id=1, replica_groups=mesh['region'=2,'tile'=4,'member'=2,'date'=2] {'member'}, dimensions={2}, use_global_device_ids=true | all-gather | bytes 98304 | tf_op jit(solution)/shard_map/all_gather | solution.py:84
  21.2 0.1 shift_right_arithmetic.26
  21.3 0.9 %copy.23 = bf16[1,8,64,512]{3,2,1,0:T(8,128)(2,1)} copy(bf16[1,8,64,512]{3,1,2,0:T(8,128)(2,1)S(1)} %bitcast.82) | data formatting | bytes 1048576
  22.3 5.1 %all-to-all-start.1 = ((bf16[4,2,2,32,512]{4,3,2,1,0:T(8,128)(2,1)}), bf16[4,2,2,32,512]{4,3,2,1,0:T(8,128)(2,1)S(1)}, u32[]{:S(2)}, u32[]{:S(2)}) async-start(bf16[4,2,2,32,512]{4,3,2,1,0:T(8,128)(2,1)} %bitcast.41), calls=%async_computation.1 | async-start | bytes 1048576 | tf_op jit(solution)/shard_map/all_to_all | solution.py:98
  27.4 0.1 shift_right_arithmetic.23
  27.5 0.1 shift_right_arithmetic.24
  27.6 0.2 copy.17
  27.9 0.1 broadcast_in_dim.101
  28.0 0.4 copy.18
  28.3 10.7 %all-to-all-done.1 = bf16[4,2,2,32,512]{4,3,2,1,0:T(8,128)(2,1)S(1)} async-done(((bf16[4,2,2,32,512]{4,3,2,1,0:T(8,128)(2,1)}), bf16[4,2,2,32,512]{4,3,2,1,0:T(8,128)(2,1)S(1)}, u32[]{:S(2)}, u32[]{:S(2)}) %all-to-all-start.1) | async-done | bytes 524320 | tf_op jit(solution)/shard_map/all_to_all | solution.py:98
  39.0 9.3 %fusion.7 = bf16[8,2,16,256]{3,2,1,0:T(8,128)(2,1)S(1)} fusion(bf16[8,2,32,512]{3,2,1,0:T(8,128)(2,1)S(1)} %bitcast.84, f32[]{:T(128)} %bitcast.27, s32[256]{0:T(256)S(1)} %get-tuple-element.20, f32[]{:T(128)} %bitcast.26, s32[256]{0:T(256)S(1)} %get-tuple-element.21, f32[]{:T(128)} %bitcast.25, s32[256]{0:T(256)S(1)} %get-tuple-element.22, f32[]{:T(128)} %bitcast.24, ...), kind=kOutput, calls=%fused_computation.12 | convolution fusion | flops 78785024 | bytes 1056248 | tf_op jit(solution)/shard_map/...ic,cj->...ij/dot_general | solution.py:49
  48.3 9.3 %convolution_convert_fusion.2 = bf16[8,2,512,32]{2,3,1,0:T(8,128)(2,1)S(1)} fusion(bf16[8,2,16,256]{3,2,1,0:T(8,128)(2,1)S(1)} %fusion.7, f32[]{:T(128)} %bitcast.27, s32[256]{0:T(256)S(1)} %get-tuple-element.20, f32[]{:T(128)} %bitcast.26, s32[256]{0:T(256)S(1)} %get-tuple-element.21, f32[]{:T(128)} %bitcast.25, s32[256]{0:T(256)S(1)} %get-tuple-element.22, ...), kind=kOutput, calls=%fused_computation.2 | convolution fusion | flops 78653952 | bytes 663032 | tf_op jit(solution)/shard_map/ir,...ic->...rc/dot_general | solution.py:58
  57.6 15.5 %all_to_all.15 = bf16[4,2,2,32,512]{4,3,2,1,0:T(8,128)(2,1)S(1)} all-to-all(bf16[4,2,2,32,512]{4,3,2,1,0:T(8,128)(2,1)S(1)} %bitcast.85), channel_id=1, replica_groups=mesh['region'=2,'tile'=4,'member'=2,'date'=2] {'tile'}, dimensions={0} | all-to-all | bytes 1048576 | tf_op jit(solution)/shard_map/all_to_all | solution.py:107
  73.1 0.2 reshape.71
  73.4 0.4 convolution_convert_fusion.1
  73.7 0.7 %copy.24 = bf16[1,4,64,512]{3,2,1,0:T(8,128)(2,1)} copy(bf16[1,4,64,512]{3,1,2,0:T(4,128)(2,1)S(1)} %bitcast.83) | data formatting | bytes 524288
  (20 shorter events, 0.1 us)
Async XLA Ops:
  0.0 0.7 copy-start.4
  0.7 0.7 copy-start.3
  2.1 20.2 %all-to-all-start = ((s32[4,2,32]{2,1,0:T(2,128)}), s32[4,2,32]{2,1,0:T(2,128)S(1)}, u32[]{:S(2)}, u32[]{:S(2)}) async-start(s32[4,2,32]{2,1,0:T(2,128)} %bitcast.4), calls=%async_computation | async-start | bytes 8192 | tf_op jit(solution)/shard_map/all_to_all | solution.py:99
  8.5 0.7 copy-start.2
  11.2 0.8 %copy-start = (bf16[1,1,4,16,256]{4,3,2,1,0:T(8,128)(2,1)S(1)}, bf16[1,1,4,16,256]{4,3,2,1,0:T(8,128)(2,1)}, u32[]{:S(2)}) copy-start(bf16[1,1,4,16,256]{4,3,2,1,0:T(8,128)(2,1)} %param.9) | copy-start | bytes 98308
  11.9 4.7 %copy-start.1 = (bf16[1,1,4,16,256]{4,3,2,1,0:T(8,128)(2,1)S(1)}, bf16[1,1,4,16,256]{4,3,2,1,0:T(8,128)(2,1)}, u32[]{:S(2)}) copy-start(bf16[1,1,4,16,256]{4,3,2,1,0:T(8,128)(2,1)} %param.10) | copy-start | bytes 98308
  22.3 16.7 %all-to-all-start.1 = ((bf16[4,2,2,32,512]{4,3,2,1,0:T(8,128)(2,1)}), bf16[4,2,2,32,512]{4,3,2,1,0:T(8,128)(2,1)S(1)}, u32[]{:S(2)}, u32[]{:S(2)}) async-start(bf16[4,2,2,32,512]{4,3,2,1,0:T(8,128)(2,1)} %bitcast.41), calls=%async_computation.1 | async-start | bytes 1048576 | tf_op jit(solution)/shard_map/all_to_all | solution.py:98
where the time goes:
time: 75.2 us; the launch traced here: 74.5 us
  blocking collectives  24.8 us (33%)
  matrix products  19.4 us (26%)
  starting transfers between devices  11.4 us (15%)
  waiting for transfers between devices  10.7 us (14%)
  local copies, waits for them, and re-layouts  6.98 us (9%)
  other arithmetic  1.09 us (1%)
    all_to_all x1, blocking collectives, per_device(): lax.all_to_all(answered, 'tile', split_axis=0, concat_axis=0, tiled=True)  15.5 us
    all_to_all x1, waiting for transfers between devices, per_device(): lax.all_to_all(outgoing, 'tile', split_axis=0, concat_axis=0, tiled=True)  10.7 us
    dot_general x1, matrix products, degrade(): jnp.einsum('...ic,cj->...ij', blurred, col_table, preferred_element_type=...  9.32 us
    dot_general x1, matrix products, adjoint_map(): jnp.einsum('ir,...ic->...rc', row_table, spread, preferred_element_type=j...  9.32 us
    all_to_all x1, starting transfers between devices, per_device(): lax.all_to_all(words_out, 'tile', split_axis=0, concat_axis=0, tiled=True)  6.32 us
    all_to_all x1, starting transfers between devices, per_device(): lax.all_to_all(outgoing, 'tile', split_axis=0, concat_axis=0, tiled=True)  5.08 us
    all_gather x1, blocking collectives, per_device(): lax.all_gather(scene_lai, 'member', axis=2, tiled=True)  4.71 us
    all_gather x1, blocking collectives, per_device(): lax.all_gather(scene_sigma, 'member', axis=2, tiled=True)  4.58 us
  transfers between devices with their start and end apart: 2, of which 1 were waited for; matrix products, arithmetic and copies ran while one was open for 6% of the time, Pallas kernels for 0%

commit v1 on v0

v1 whole, which is shorter than its diff:
```python
import math

import jax
import jax.numpy as jnp
import numpy as np
from jax import lax
from jax.experimental import pallas as pl
from jax.experimental.pallas import tpu as pltpu
from jax.sharding import PartitionSpec as P

CAP = 2
GROUP = ("tile", "member")


def plan(n_tile, n_mem):
    per = n_tile // n_mem
    steps = []
    table = np.zeros((n_tile * n_mem, n_tile), np.int32)
    for k in range(per):
        for j in range(n_mem):
            pairs, block = [], np.zeros((n_tile * n_mem,), np.int32)
            for o in range(n_tile):
                for mm in range(n_mem):
                    a = (o % per + k) % per
                    m = (o // per + j) % n_mem
                    s = mm * per + a
                    pairs.append((o * n_mem + mm, s * n_mem + m))
                    block[o * n_mem + mm] = a
                    table[s * n_mem + m, o] = len(steps)
            steps.append((pairs, block))
    return steps, table


def chunk_tiles(tiles, members, rows):
    best = 1
    for c in range(1, tiles + 1):
        if tiles % c == 0 and c * members * rows <= 256:
            best = c
    return best


def iota(shape, dim):
    return lax.broadcasted_iota(jnp.int32, shape, dim)


def pick(which, taps, row):
    out = jnp.zeros(which.shape, jnp.float32)
    for k in range(taps.shape[1]):
        out = jnp.where(which == k, taps[row : row + 1, k : k + 1], out)
    return out.astype(jnp.bfloat16)


def before(sizes, taps_ref, words_ref, field_ref, pred_ref, valid_ref, colt_ref, rowt_ref, pad):
    tiles, chunk, members, rows, cols = sizes
    half_r, half_c = rows // 2, cols // 2
    n_words = words_ref.shape[1]
    taps = taps_ref[...]
    taps = taps / jnp.sum(taps, axis=1, keepdims=True)
    reach = taps.shape[1] // 2
    fields = chunk * members
    fr, fh = fields * rows, fields * half_r
    i, r = iota((fh, fr), 0), iota((fh, fr), 1)
    row_bd = jnp.where(
        i // half_r == r // rows, r % rows - 2 * (i % half_r) + reach, -1
    )
    row_bd = pick(row_bd, taps, 0)
    i, r = iota((fr, fh), 1), iota((fr, fh), 0)
    rowt = jnp.where(i // half_r == r // rows, r % rows - 2 * (i % half_r) + reach, -1)
    rowt_ref[...] = pick(rowt, taps, 0)
    col = pick(iota((cols, half_c), 0) - 2 * iota((cols, half_c), 1) + reach, taps, 1)
    colt_ref[...] = pick(iota((half_c, cols), 1) - 2 * iota((half_c, cols), 0) + reach, taps, 1)
    for g in range(tiles // chunk):
        field = field_ref[g * fr : (g + 1) * fr, :]
        blurred = jnp.dot(row_bd, field, preferred_element_type=jnp.float32).astype(jnp.bfloat16)
        pred_ref[g * fh : (g + 1) * fh, :] = jnp.dot(
            blurred, col, preferred_element_type=jnp.float32
        ).astype(jnp.bfloat16)
    pad[...] = jnp.zeros(pad.shape, jnp.int32)
    pad[:, :n_words] = words_ref[...]
    per_row = half_c // 2 // 32
    for t in range(tiles):
        words = jnp.broadcast_to(pad[t : t + 1, :], (8, 128))
        for i0 in range(0, half_r, 8):
            for j0 in range(0, half_c, 128):
                i = iota((8, 128), 0) + i0
                j = iota((8, 128), 1) + j0
                word = jnp.take_along_axis(words, i // 2 * per_row + j // 64, axis=1)
                bit = jnp.bitwise_and(jnp.right_shift(word, j // 2 % 32), 1)
                valid_ref[t * half_r + i0 : t * half_r + i0 + 8, j0 : j0 + 128] = bit.astype(jnp.float32)


def after(sizes, n_steps, owners_ref, table_ref, pred_ref, valid_ref, colt_ref, rowt_ref, *refs):
    tiles, chunk, members, rows, cols = sizes
    half_r, half_c = rows // 2, cols // 2
    arrived, out_ref, scenes = refs[:n_steps], refs[n_steps], refs[n_steps + 1]
    fields = chunk * members
    fr, fh = fields * rows, fields * half_r
    device = lax.axis_index(GROUP)
    for p in range(n_steps):
        scenes[p] = arrived[p][...]
    owner = [owners_ref[0, t] for t in range(tiles)]
    for g in range(tiles // chunk):
        parts = []
        for t in range(g * chunk, (g + 1) * chunk):
            rank = 0
            for u in range(t):
                rank = rank + jnp.where(owner[u] == owner[t], 1, 0)
            step = table_ref[device, owner[t]]
            seen = scenes[step, 0, rank].astype(jnp.float32)
            sigma = scenes[step, 1, rank].astype(jnp.float32)
            weight = valid_ref[t * half_r : (t + 1) * half_r, :] / (sigma * sigma)
            for m in range(members):
                at = (t * members + m) * half_r
                gap = seen - pred_ref[at : at + half_r, :].astype(jnp.float32)
                parts.append((gap * weight).astype(jnp.bfloat16))
        misfit = jnp.concatenate(parts, axis=0)
        spread = jnp.dot(misfit, colt_ref[...], preferred_element_type=jnp.float32).astype(jnp.bfloat16)
        out_ref[g * fr : (g + 1) * fr, :] = jnp.dot(
            rowt_ref[...], spread, preferred_element_type=jnp.float32
        ).astype(jnp.bfloat16)


def per_device(sim_lai, owner_ids, cloud_words, scene_lai, scene_sigma, mtf_taps):
    n_tile, n_mem = lax.axis_size("tile"), lax.axis_size("member")
    _, tiles, members, rows, cols = sim_lai.shape
    half_r, half_c = rows // 2, cols // 2
    steps, table = plan(n_tile, n_mem)
    per = n_tile // n_mem
    both = jnp.stack([scene_lai[0, 0], scene_sigma[0, 0]], 0)
    device = lax.axis_index(GROUP)
    blocks = {}
    arrived = []
    for pairs, block in steps:
        key = tuple(block)
        if key not in blocks:
            a = jnp.asarray(block)[device]
            blocks[key] = lax.dynamic_slice_in_dim(both, a * CAP, CAP, 1)
        arrived.append(lax.ppermute(blocks[key], GROUP, pairs))
    chunk = chunk_tiles(tiles, members, rows)
    sizes = (tiles, chunk, members, rows, cols)
    fields = chunk * members
    fr, fh = fields * rows, fields * half_r
    vmem = pl.BlockSpec(memory_space=pltpu.VMEM)
    smem = pl.BlockSpec(memory_space=pltpu.SMEM)
    pred, valid, colt, rowt = pl.pallas_call(
        lambda *refs: before(sizes, *refs),
        out_shape=(
            jax.ShapeDtypeStruct((tiles * members * half_r, half_c), jnp.bfloat16),
            jax.ShapeDtypeStruct((tiles * half_r, half_c), jnp.float32),
            jax.ShapeDtypeStruct((half_c, cols), jnp.bfloat16),
            jax.ShapeDtypeStruct((fr, fh), jnp.bfloat16),
        ),
        in_specs=[vmem] * 3,
        out_specs=[vmem] * 4,
        scratch_shapes=[pltpu.VMEM((tiles, 128), jnp.int32)],
        name="before",
    )(mtf_taps, cloud_words[0], sim_lai.reshape(tiles * members * rows, cols))
    out = pl.pallas_call(
        lambda *refs: after(sizes, len(steps), *refs),
        out_shape=jax.ShapeDtypeStruct((tiles * members * rows, cols), jnp.bfloat16),
        in_specs=[smem, smem] + [vmem] * (4 + len(steps)),
        out_specs=vmem,
        scratch_shapes=[pltpu.VMEM((len(steps), 2, CAP, half_r, half_c), jnp.bfloat16)],
        name="after",
    )(owner_ids, jnp.asarray(table), pred, valid, colt, rowt, *arrived)
    return out.reshape(sim_lai.shape)


def solution(mesh):
    placed = (
        P("date", ("region", "tile"), "member", None, None),
        P("date", ("region", "tile")),
        P("date", ("region", "tile"), None),
        P("date", ("region", "tile"), "member", None, None),
        P("date", ("region", "tile"), "member", None, None),
        P(),
    )
    return jax.shard_map(
        per_device,
        mesh=mesh,
        in_specs=placed,
        out_specs=P("date", ("region", "tile"), "member", None, None),
        check_vma=False,
    )
```

time: 75.2 us -> 20.4 us (0.27)
  the two profiles are of different devices: /device:TPU:0 before, /device:TPU:6 now
where the time goes in v1:
time: 20.4 us; the launch traced here: 20 us
  starting transfers between devices  8.9 us (44%)
  Pallas kernels  5.05 us (25%)
  local copies, waits for them, and re-layouts  2.45 us (12%)
  waiting for transfers between devices  1.49 us (7%)
  between operations  1.39 us (7%)
  other arithmetic  0.75 us (4%)
    ppermute x4, starting transfers between devices, per_device(): arrived.append(lax.ppermute(blocks[key], GROUP, pairs))  8.9 us
    pallas_call x1, Pallas kernels, per_device(): pl.pallas_call(lambda *refs: before(sizes, *refs), out_shape=(jax.ShapeDt...  2.85 us
    pallas_call x1, Pallas kernels, per_device(): pl.pallas_call(lambda *refs: after(sizes, len(steps), *refs), out_shape=j...  2.2 us
    ppermute x4, waiting for transfers between devices, per_device(): arrived.append(lax.ppermute(blocks[key], GROUP, pairs))  1.49 us
    unnamed x14, local copies, waits for them, and re-layouts  1.25 us
    dynamic_slice x2, local copies, waits for them, and re-layouts, per_device(): a = jnp.asarray(block)[device]  1.19 us
    another operation x1, other arithmetic, per_device(): both = jnp.stack([scene_lai[0, 0], scene_sigma[0, 0]], 0)  0.75 us
  transfers between devices with their start and end apart: 4, of which 1 were waited for; matrix products, arithmetic and copies ran while one was open for 0% of the time, Pallas kernels for 14%

profile of v1, /device:TPU:6, one launch (start us, length us, event | category | flops | bytes accessed | tf_op | source)
XLA Modules:
  0.0 20.0 jit_solution(10353907337578582931)
XLA Ops:
  0.0 0.0 copy-start.6
  0.0 0.0 copy-start.5
  0.0 0.0 copy-start.4
  0.0 0.6 %copy-done.6 = s32[8]{0:T(128)S(1)} copy-done((s32[8]{0:T(128)S(1)}, s32[8]{0:T(128)}, u32[]{:S(2)}) %copy-start.6) | copy-done | bytes 56
  0.7 0.6 %dynamic_slice.14 = s32[1]{0:T(128)} dynamic-slice(s32[8]{0:T(128)S(1)} %copy-done.6, s32[]{:T(128)S(6)} %select_n.10), dynamic_slice_sizes={1} | dynamic-slice | bytes 12 | tf_op jit(solution)/shard_map/dynamic_slice | solution.py:136
  1.9 0.0 copy-done.5
  1.9 0.6 %dynamic_slice.12 = s32[1]{0:T(128)} dynamic-slice(s32[8]{0:T(128)S(1)} %copy-done.5, s32[]{:T(128)S(6)} %select_n.10), dynamic_slice_sizes={1} | dynamic-slice | bytes 12 | tf_op jit(solution)/shard_map/dynamic_slice | solution.py:136
  3.2 0.0 copy-done.4
  3.2 0.7 %fusion = (bf16[2,2,16,256]{3,2,1,0:T(8,128)(2,1)S(1)}, bf16[2,2,16,256]{3,2,1,0:T(8,128)(2,1)S(1)}) fusion(s32[]{:T(128)S(6)} %select_n.12, bf16[1,4,16,256]{3,2,1,0:T(8,128)(2,1)S(1)} %bitcast.8, bf16[1,4,16,256]{3,2,1,0:T(8,128)(2,1)} %bitcast.9, s32[]{:T(128)S(6)} %select_n.11), kind=kLoop, calls=%fused_computation.4 | loop fusion | flops 32768 | bytes 131080 | tf_op jit(solution)/shard_map/stack | solution.py:129
  3.9 3.6 %collective-permute-start.2 = (bf16[2,2,16,256]{3,2,1,0:T(8,128)(2,1)S(1)}, bf16[2,2,16,256]{3,2,1,0:T(8,128)(2,1)S(1)}, u32[]{:S(2)}, u32[]{:S(2)}) collective-permute-start(bf16[2,2,16,256]{3,2,1,0:T(8,128)(2,1)S(1)} %get-tuple-element.13), channel_id=1, source_target_pairs={{0,4},{2,12},{4,0},{6,8},{8,6},{10,14},{12,2},{14,10},{1,5},{3,13}... | collective-permute-start | bytes 98312 | tf_op jit(solution)/shard_map/ppermute | solution.py:138
  7.6 0.5 %collective-permute-start.3 = (bf16[2,2,16,256]{3,2,1,0:T(8,128)(2,1)S(1)}, bf16[2,2,16,256]{3,2,1,0:T(8,128)(2,1)S(1)}, u32[]{:S(2)}, u32[]{:S(2)}) collective-permute-start(bf16[2,2,16,256]{3,2,1,0:T(8,128)(2,1)S(1)} %get-tuple-element.13), channel_id=1, source_target_pairs={{0,6},{2,14},{4,2},{6,10},{8,4},{10,12},{12,0},{14,8},{1,7},{3,15}... | collective-permute-start | bytes 98312 | tf_op jit(solution)/shard_map/ppermute | solution.py:138
  8.0 1.2 %collective-permute-start.1 = (bf16[2,2,16,256]{3,2,1,0:T(8,128)(2,1)S(1)}, bf16[2,2,16,256]{3,2,1,0:T(8,128)(2,1)S(1)}, u32[]{:S(2)}, u32[]{:S(2)}) collective-permute-start(bf16[2,2,16,256]{3,2,1,0:T(8,128)(2,1)S(1)} %get-tuple-element.14), channel_id=1, source_target_pairs={{0,2},{2,10},{4,6},{6,14},{8,0},{10,8},{12,4},{14,12},{1,3},{3,11}... | collective-permute-start | bytes 98312 | tf_op jit(solution)/shard_map/ppermute | solution.py:138
  9.3 3.6 %collective-permute-start = (bf16[2,2,16,256]{3,2,1,0:T(8,128)(2,1)S(1)}, bf16[2,2,16,256]{3,2,1,0:T(8,128)(2,1)S(1)}, u32[]{:S(2)}, u32[]{:S(2)}) collective-permute-start(bf16[2,2,16,256]{3,2,1,0:T(8,128)(2,1)S(1)} %get-tuple-element.14), channel_id=1, source_target_pairs={{0,0},{2,8},{4,4},{6,12},{8,2},{10,10},{12,6},{14,14},{1,1},{3,9},... | collective-permute-start | bytes 98312 | tf_op jit(solution)/shard_map/ppermute | solution.py:138
  12.8 2.8 %before.1 = (bf16[128,256]{1,0:T(8,128)(2,1)}, f32[64,256]{1,0:T(8,128)}, bf16[256,512]{1,0:T(8,128)(2,1)}, bf16[256,128]{1,0:T(8,128)(2,1)}) custom-call(f32[2,7]{1,0:T(2,128)} %refs_0_.2, s32[4,32]{1,0:T(4,128)} %bitcast.10, bf16[256,512]{1,0:T(8,128)(2,1)} %bitcast.7), custom_call_target="tpu_custom_call" | custom-call | tf_op jit(solution)/shard_map/before/pallas_call | solution.py:145
  15.7 0.0 collective-permute-done.2.refs_8_
  15.7 0.0 copy-start
  15.7 0.0 collective-permute-done.3.refs_9_
  15.7 0.0 copy-start.1
  15.7 0.0 collective-permute-done.1.refs_7_
  15.7 0.0 copy-start.2
  15.7 1.5 %collective-permute-done.refs_6_ = bf16[2,2,16,256]{3,2,1,0:T(8,128)(2,1)S(1)} collective-permute-done((bf16[2,2,16,256]{3,2,1,0:T(8,128)(2,1)S(1)}, bf16[2,2,16,256]{3,2,1,0:T(8,128)(2,1)S(1)}, u32[]{:S(2)}, u32[]{:S(2)}) %collective-permute-start) | collective-permute-done | bytes 32800 | tf_op jit(solution)/shard_map/ppermute | solution.py:138
  17.2 0.0 copy-start.3
  17.2 0.0 copy-done
  17.2 0.0 copy-done.1
  17.2 0.0 copy-done.2
  17.2 0.6 %copy-done.3 = bf16[2,2,16,256]{3,2,1,0:T(8,128)(2,1)} copy-done((bf16[2,2,16,256]{3,2,1,0:T(8,128)(2,1)}, bf16[2,2,16,256]{3,2,1,0:T(8,128)(2,1)S(1)}, u32[]{:S(2)}) %copy-start.3) | copy-done | bytes 32792
  17.8 2.2 %after.1 = bf16[256,512]{1,0:T(8,128)(2,1)} custom-call(s32[1,4]{1,0:T(1,128)} %refs_0_.3, s32[8,4]{1,0:T(8,128)} %constant.28.clone.refs_1_, bf16[128,256]{1,0:T(8,128)(2,1)} %get-tuple-element.9.refs_2_, f32[64,256]{1,0:T(8,128)} %get-tuple-element.10.refs_3_, bf16[256,512]{1,0:T(8,128)(2,1)} %get-tuple-element.11.refs_4_, ...), custom_call_target="tpu_custom_call" | custom-call | tf_op jit(solution)/shard_map/after/pallas_call | solution.py:158
Async XLA Ops:
  0.0 0.7 %copy-start.6 = (s32[8]{0:T(128)S(1)}, s32[8]{0:T(128)}, u32[]{:S(2)}) copy-start(s32[8]{0:T(128)} %constant.27.clone) | copy-start | bytes 100
  0.0 1.9 %copy-start.5 = (s32[8]{0:T(128)S(1)}, s32[8]{0:T(128)}, u32[]{:S(2)}) copy-start(s32[8]{0:T(128)} %constant.26.clone) | copy-start | bytes 100
  0.0 3.2 %copy-start.4 = (bf16[1,1,4,16,256]{4,3,2,1,0:T(8,128)(2,1)S(1)}, bf16[1,1,4,16,256]{4,3,2,1,0:T(8,128)(2,1)}, u32[]{:S(2)}) copy-start(bf16[1,1,4,16,256]{4,3,2,1,0:T(8,128)(2,1)} %param.12) | copy-start | bytes 98308
  3.9 11.8 %collective-permute-start.2 = (bf16[2,2,16,256]{3,2,1,0:T(8,128)(2,1)S(1)}, bf16[2,2,16,256]{3,2,1,0:T(8,128)(2,1)S(1)}, u32[]{:S(2)}, u32[]{:S(2)}) collective-permute-start(bf16[2,2,16,256]{3,2,1,0:T(8,128)(2,1)S(1)} %get-tuple-element.13), channel_id=1, source_target_pairs={{0,4},{2,12},{4,0},{6,8},{8,6},{10,14},{12,2},{14,10},{1,5},{3,13}... | collective-permute-start | bytes 98312 | tf_op jit(solution)/shard_map/ppermute | solution.py:138
  7.6 8.1 %collective-permute-start.3 = (bf16[2,2,16,256]{3,2,1,0:T(8,128)(2,1)S(1)}, bf16[2,2,16,256]{3,2,1,0:T(8,128)(2,1)S(1)}, u32[]{:S(2)}, u32[]{:S(2)}) collective-permute-start(bf16[2,2,16,256]{3,2,1,0:T(8,128)(2,1)S(1)} %get-tuple-element.13), channel_id=1, source_target_pairs={{0,6},{2,14},{4,2},{6,10},{8,4},{10,12},{12,0},{14,8},{1,7},{3,15}... | collective-permute-start | bytes 98312 | tf_op jit(solution)/shard_map/ppermute | solution.py:138
  8.0 7.7 %collective-permute-start.1 = (bf16[2,2,16,256]{3,2,1,0:T(8,128)(2,1)S(1)}, bf16[2,2,16,256]{3,2,1,0:T(8,128)(2,1)S(1)}, u32[]{:S(2)}, u32[]{:S(2)}) collective-permute-start(bf16[2,2,16,256]{3,2,1,0:T(8,128)(2,1)S(1)} %get-tuple-element.14), channel_id=1, source_target_pairs={{0,2},{2,10},{4,6},{6,14},{8,0},{10,8},{12,4},{14,12},{1,3},{3,11}... | collective-permute-start | bytes 98312 | tf_op jit(solution)/shard_map/ppermute | solution.py:138
  9.3 7.9 %collective-permute-start = (bf16[2,2,16,256]{3,2,1,0:T(8,128)(2,1)S(1)}, bf16[2,2,16,256]{3,2,1,0:T(8,128)(2,1)S(1)}, u32[]{:S(2)}, u32[]{:S(2)}) collective-permute-start(bf16[2,2,16,256]{3,2,1,0:T(8,128)(2,1)S(1)} %get-tuple-element.14), channel_id=1, source_target_pairs={{0,0},{2,8},{4,4},{6,12},{8,2},{10,10},{12,6},{14,14},{1,1},{3,9},... | collective-permute-start | bytes 98312 | tf_op jit(solution)/shard_map/ppermute | solution.py:138
  15.7 1.5 %copy-start = (bf16[2,2,16,256]{3,2,1,0:T(8,128)(2,1)}, bf16[2,2,16,256]{3,2,1,0:T(8,128)(2,1)S(1)}, u32[]{:S(2)}) copy-start(bf16[2,2,16,256]{3,2,1,0:T(8,128)(2,1)S(1)} %collective-permute-done.2.refs_8_) | copy-start | bytes 98308
  15.7 1.5 %copy-start.1 = (bf16[2,2,16,256]{3,2,1,0:T(8,128)(2,1)}, bf16[2,2,16,256]{3,2,1,0:T(8,128)(2,1)S(1)}, u32[]{:S(2)}) copy-start(bf16[2,2,16,256]{3,2,1,0:T(8,128)(2,1)S(1)} %collective-permute-done.3.refs_9_) | copy-start | bytes 98308
  15.7 1.5 %copy-start.2 = (bf16[2,2,16,256]{3,2,1,0:T(8,128)(2,1)}, bf16[2,2,16,256]{3,2,1,0:T(8,128)(2,1)S(1)}, u32[]{:S(2)}) copy-start(bf16[2,2,16,256]{3,2,1,0:T(8,128)(2,1)S(1)} %collective-permute-done.1.refs_7_) | copy-start | bytes 98308
  17.2 0.6 %copy-start.3 = (bf16[2,2,16,256]{3,2,1,0:T(8,128)(2,1)}, bf16[2,2,16,256]{3,2,1,0:T(8,128)(2,1)S(1)}, u32[]{:S(2)}) copy-start(bf16[2,2,16,256]{3,2,1,0:T(8,128)(2,1)S(1)} %collective-permute-done.refs_6_) | copy-start | bytes 98308

commit v2 on v1

--- a/solution.py
+++ b/solution.py
@@ -1,8 +1,5 @@
-import math
-
 import jax
 import jax.numpy as jnp
-import numpy as np
 from jax import lax
 from jax.experimental import pallas as pl
 from jax.experimental.pallas import tpu as pltpu
@@ -15,20 +12,17 @@
 def plan(n_tile, n_mem):
     per = n_tile // n_mem
     steps = []
-    table = np.zeros((n_tile * n_mem, n_tile), np.int32)
     for k in range(per):
         for j in range(n_mem):
-            pairs, block = [], np.zeros((n_tile * n_mem,), np.int32)
+            pairs = []
             for o in range(n_tile):
                 for mm in range(n_mem):
-                    a = (o % per + k) % per
+                    s = mm * per + (o + k) % per
                     m = (o // per + j) % n_mem
-                    s = mm * per + a
-                    pairs.append((o * n_mem + mm, s * n_mem + m))
-                    block[o * n_mem + mm] = a
-                    table[s * n_mem + m, o] = len(steps)
-            steps.append((pairs, block))
-    return steps, table
+                    if (s, m) != (o, mm):
+                        pairs.append((o * n_mem + mm, s * n_mem + m))
+            steps.append((k, j, pairs))
+    return steps
 
 
 def chunk_tiles(tiles, members, rows):
@@ -89,15 +83,18 @@
                 valid_ref[t * half_r + i0 : t * half_r + i0 + 8, j0 : j0 + 128] = bit.astype(jnp.float32)
 
 
-def after(sizes, n_steps, owners_ref, table_ref, pred_ref, valid_ref, colt_ref, rowt_ref, *refs):
+def after(sizes, ring, owners_ref, pred_ref, valid_ref, colt_ref, rowt_ref, own_ref, *refs):
     tiles, chunk, members, rows, cols = sizes
+    n_tile, n_mem = ring
+    per = n_tile // n_mem
     half_r, half_c = rows // 2, cols // 2
-    arrived, out_ref, scenes = refs[:n_steps], refs[n_steps], refs[n_steps + 1]
+    arrived, out_ref, scenes = refs[:n_tile], refs[n_tile], refs[n_tile + 1]
     fields = chunk * members
     fr, fh = fields * rows, fields * half_r
-    device = lax.axis_index(GROUP)
-    for p in range(n_steps):
+    here, member = lax.axis_index("tile"), lax.axis_index("member")
+    for p in range(n_tile):
         scenes[p] = arrived[p][...]
+    scenes[n_tile] = own_ref[...]
     owner = [owners_ref[0, t] for t in range(tiles)]
     for g in range(tiles // chunk):
         parts = []
@@ -105,7 +102,10 @@
             rank = 0
             for u in range(t):
                 rank = rank + jnp.where(owner[u] == owner[t], 1, 0)
-            step = table_ref[device, owner[t]]
+            k = (here - owner[t]) % per
+            j = (member - owner[t] // per) % n_mem
+            mine = jnp.logical_and(owner[t] == here, here // per == member)
+            step = jnp.where(mine, n_tile, k * n_mem + j)
             seen = scenes[step, 0, rank].astype(jnp.float32)
             sigma = scenes[step, 1, rank].astype(jnp.float32)
             weight = valid_ref[t * half_r : (t + 1) * half_r, :] / (sigma * sigma)
@@ -124,18 +124,13 @@
     n_tile, n_mem = lax.axis_size("tile"), lax.axis_size("member")
     _, tiles, members, rows, cols = sim_lai.shape
     half_r, half_c = rows // 2, cols // 2
-    steps, table = plan(n_tile, n_mem)
     per = n_tile // n_mem
     both = jnp.stack([scene_lai[0, 0], scene_sigma[0, 0]], 0)
-    device = lax.axis_index(GROUP)
-    blocks = {}
-    arrived = []
-    for pairs, block in steps:
-        key = tuple(block)
-        if key not in blocks:
-            a = jnp.asarray(block)[device]
-            blocks[key] = lax.dynamic_slice_in_dim(both, a * CAP, CAP, 1)
-        arrived.append(lax.ppermute(blocks[key], GROUP, pairs))
+    here = lax.axis_index("tile")
+    blocks = [lax.dynamic_slice_in_dim(both, (here + k) % per * CAP, CAP, 1) for k in range(per)]
+    own = blocks[0]
+    arrived = [lax.ppermute(blocks[k], GROUP, pairs) for k, j, pairs in plan(n_tile, n_mem)]
+    arrived = [pltpu.with_memory_space_constraint(x, pltpu.VMEM) for x in arrived]
     chunk = chunk_tiles(tiles, members, rows)
     sizes = (tiles, chunk, members, rows, cols)
     fields = chunk * members
@@ -145,24 +140,25 @@
     pred, valid, colt, rowt = pl.pallas_call(
         lambda *refs: before(sizes, *refs),
         out_shape=(
-            jax.ShapeDtypeStruct((tiles * members * half_r, half_c), jnp.bfloat16),
-            jax.ShapeDtypeStruct((tiles * half_r, half_c), jnp.float32),
-            jax.ShapeDtypeStruct((half_c, cols), jnp.bfloat16),
-            jax.ShapeDtypeStruct((fr, fh), jnp.bfloat16),
+            pltpu.VMEM((tiles * members * half_r, half_c), jnp.bfloat16),
+            pltpu.VMEM((tiles * half_r, half_c), jnp.float32),
+            pltpu.VMEM((half_c, cols), jnp.bfloat16),
+            pltpu.VMEM((fr, fh), jnp.bfloat16),
         ),
         in_specs=[vmem] * 3,
         out_specs=[vmem] * 4,
         scratch_shapes=[pltpu.VMEM((tiles, 128), jnp.int32)],
         name="before",
     )(mtf_taps, cloud_words[0], sim_lai.reshape(tiles * members * rows, cols))
+    resident = [pltpu.with_memory_space_constraint(x, pltpu.VMEM) for x in (pred, valid, colt, rowt, own)]
     out = pl.pallas_call(
-        lambda *refs: after(sizes, len(steps), *refs),
+        lambda *refs: after(sizes, (n_tile, n_mem), *refs),
         out_shape=jax.ShapeDtypeStruct((tiles * members * rows, cols), jnp.bfloat16),
-        in_specs=[smem, smem] + [vmem] * (4 + len(steps)),
+        in_specs=[smem] + [vmem] * (5 + n_tile),
         out_specs=vmem,
-        scratch_shapes=[pltpu.VMEM((len(steps), 2, CAP, half_r, half_c), jnp.bfloat16)],
+        scratch_shapes=[pltpu.VMEM((n_tile + 1, 2, CAP, half_r, half_c), jnp.bfloat16)],
         name="after",
-    )(owner_ids, jnp.asarray(table), pred, valid, colt, rowt, *arrived)
+    )(owner_ids, *resident, *arrived)
     return out.reshape(sim_lai.shape)
 
 

time: 20.4 us -> 16.1 us (0.79)
  the two profiles are of different devices: /device:TPU:6 before, /device:TPU:2 now
where the time goes in v2:
time: 16.1 us; the launch traced here: 15.9 us
  starting transfers between devices  8.9 us (55%)
  Pallas kernels  3.92 us (24%)
  waiting for transfers between devices  2.22 us (14%)
  local copies, waits for them, and re-layouts  0.77 us (5%)
    ppermute x4, starting transfers between devices, per_device(): lax.ppermute(blocks[k], GROUP, pairs)  8.9 us
    ppermute x4, waiting for transfers between devices, per_device(): lax.ppermute(blocks[k], GROUP, pairs)  2.22 us
    pallas_call x1, Pallas kernels, per_device(): pl.pallas_call(lambda *refs: before(sizes, *refs), out_shape=(pltpu.VMEM(...  2.13 us
    pallas_call x1, Pallas kernels, per_device(): pl.pallas_call(lambda *refs: after(sizes, (n_tile, n_mem), *refs), out_sh...  1.78 us
    unnamed x4, local copies, waits for them, and re-layouts  0.77 us
  transfers between devices with their start and end apart: 4, of which 1 were waited for; matrix products, arithmetic and copies ran while one was open for 0% of the time, Pallas kernels for 13%

profile of v2, /device:TPU:2, one launch (start us, length us, event | category | flops | bytes accessed | tf_op | source)
XLA Modules:
  0.0 15.9 jit_solution(4044605912097153423)
XLA Ops:
  0.0 0.0 copy-start.1
  0.0 0.0 copy-start
  0.0 0.8 %copy-done.1 = bf16[1,1,4,16,256]{4,3,2,1,0:T(8,128)(2,1)S(1)} copy-done((bf16[1,1,4,16,256]{4,3,2,1,0:T(8,128)(2,1)S(1)}, bf16[1,1,4,16,256]{4,3,2,1,0:T(8,128)(2,1)}, u32[]{:S(2)}) %copy-start.1) | copy-done | bytes 32792
  0.8 0.0 copy-done
  0.8 3.6 %collective-permute-start.2 = (bf16[2,2,16,256]{3,2,1,0:T(8,128)(2,1)S(1)}, bf16[2,2,16,256]{3,2,1,0:T(8,128)(2,1)S(1)}, u32[]{:S(2)}, u32[]{:S(2)}) collective-permute-start(bf16[2,2,16,256]{3,2,1,0:T(8,128)(2,1)S(1)} %get-tuple-element.13), channel_id=1, source_target_pairs={{0,4},{2,12},{4,0},{6,8},{8,6},{10,14},{12,2},{14,10},{1,5},{3,13}... | collective-permute-start | bytes 98312 | tf_op jit(solution)/shard_map/ppermute | solution.py:132
  4.4 0.5 %collective-permute-start.3 = (bf16[2,2,16,256]{3,2,1,0:T(8,128)(2,1)S(1)}, bf16[2,2,16,256]{3,2,1,0:T(8,128)(2,1)S(1)}, u32[]{:S(2)}, u32[]{:S(2)}) collective-permute-start(bf16[2,2,16,256]{3,2,1,0:T(8,128)(2,1)S(1)} %get-tuple-element.13), channel_id=1, source_target_pairs={{0,6},{2,14},{4,2},{6,10},{8,4},{10,12},{12,0},{14,8},{1,7},{3,15}... | collective-permute-start | bytes 98312 | tf_op jit(solution)/shard_map/ppermute | solution.py:132
  4.9 1.2 %collective-permute-start.1 = (bf16[2,2,16,256]{3,2,1,0:T(8,128)(2,1)S(1)}, bf16[2,2,16,256]{3,2,1,0:T(8,128)(2,1)S(1)}, u32[]{:S(2)}, u32[]{:S(2)}) collective-permute-start(bf16[2,2,16,256]{3,2,1,0:T(8,128)(2,1)S(1)} %get-tuple-element.14.refs_5_), channel_id=1, source_target_pairs={{0,2},{2,10},{4,6},{6,14},{8,0},{10,8},{12,4},{14,12},{1,3},{3,11}... | collective-permute-start | bytes 98312 | tf_op jit(solution)/shard_map/ppermute | solution.py:132
  6.1 3.6 %collective-permute-start = (bf16[2,2,16,256]{3,2,1,0:T(8,128)(2,1)S(1)}, bf16[2,2,16,256]{3,2,1,0:T(8,128)(2,1)S(1)}, u32[]{:S(2)}, u32[]{:S(2)}) collective-permute-start(bf16[2,2,16,256]{3,2,1,0:T(8,128)(2,1)S(1)} %get-tuple-element.14.refs_5_), channel_id=1, source_target_pairs={{2,8},{6,12},{8,2},{12,6},{3,9},{7,13},{9,3},{13,7},{18,24},{22,28... | collective-permute-start | bytes 98312 | tf_op jit(solution)/shard_map/ppermute | solution.py:132
  9.7 2.1 %before.1 = (bf16[128,256]{1,0:T(8,128)(2,1)S(1)}, f32[64,256]{1,0:T(8,128)S(1)}, bf16[256,512]{1,0:T(8,128)(2,1)S(1)}, bf16[256,128]{1,0:T(8,128)(2,1)S(1)}) custom-call(f32[2,7]{1,0:T(2,128)} %refs_0_.2, s32[4,32]{1,0:T(4,128)} %bitcast.8, bf16[256,512]{1,0:T(8,128)(2,1)} %bitcast.5), custom_call_target="tpu_custom_call" | custom-call | tf_op jit(solution)/shard_map/before/pallas_call | solution.py:140
  11.8 0.0 collective-permute-done.2.refs_8_
  11.8 0.0 collective-permute-done.3.refs_9_
  11.9 0.0 collective-permute-done.1.refs_7_
  11.9 2.2 %collective-permute-done.refs_6_ = bf16[2,2,16,256]{3,2,1,0:T(8,128)(2,1)S(1)} collective-permute-done((bf16[2,2,16,256]{3,2,1,0:T(8,128)(2,1)S(1)}, bf16[2,2,16,256]{3,2,1,0:T(8,128)(2,1)S(1)}, u32[]{:S(2)}, u32[]{:S(2)}) %collective-permute-start) | collective-permute-done | bytes 32800 | tf_op jit(solution)/shard_map/ppermute | solution.py:132
  14.1 1.8 %after.1 = bf16[256,512]{1,0:T(8,128)(2,1)} custom-call(s32[1,4]{1,0:T(1,128)} %refs_0_.3, bf16[128,256]{1,0:T(8,128)(2,1)S(1)} %get-tuple-element.9.refs_1_, f32[64,256]{1,0:T(8,128)S(1)} %get-tuple-element.10.refs_2_, bf16[256,512]{1,0:T(8,128)(2,1)S(1)} %get-tuple-element.11.refs_3_, bf16[256,128]{1,0:T(8,128)(2,1)S(1)} %get-tuple-element.12.refs_4_, ...), custom_call_target="tpu_custom_call" | custom-call | tf_op jit(solution)/shard_map/after/pallas_call | solution.py:154
  (1 shorter events, 0.0 us)
Async XLA Ops:
  0.0 0.8 %copy-start.1 = (bf16[1,1,4,16,256]{4,3,2,1,0:T(8,128)(2,1)S(1)}, bf16[1,1,4,16,256]{4,3,2,1,0:T(8,128)(2,1)}, u32[]{:S(2)}) copy-start(bf16[1,1,4,16,256]{4,3,2,1,0:T(8,128)(2,1)} %param.10) | copy-start | bytes 98308
  0.0 0.8 %copy-start = (bf16[1,1,4,16,256]{4,3,2,1,0:T(8,128)(2,1)S(1)}, bf16[1,1,4,16,256]{4,3,2,1,0:T(8,128)(2,1)}, u32[]{:S(2)}) copy-start(bf16[1,1,4,16,256]{4,3,2,1,0:T(8,128)(2,1)} %param.9) | copy-start | bytes 98308
  0.8 11.1 %collective-permute-start.2 = (bf16[2,2,16,256]{3,2,1,0:T(8,128)(2,1)S(1)}, bf16[2,2,16,256]{3,2,1,0:T(8,128)(2,1)S(1)}, u32[]{:S(2)}, u32[]{:S(2)}) collective-permute-start(bf16[2,2,16,256]{3,2,1,0:T(8,128)(2,1)S(1)} %get-tuple-element.13), channel_id=1, source_target_pairs={{0,4},{2,12},{4,0},{6,8},{8,6},{10,14},{12,2},{14,10},{1,5},{3,13}... | collective-permute-start | bytes 98312 | tf_op jit(solution)/shard_map/ppermute | solution.py:132
  4.4 7.4 %collective-permute-start.3 = (bf16[2,2,16,256]{3,2,1,0:T(8,128)(2,1)S(1)}, bf16[2,2,16,256]{3,2,1,0:T(8,128)(2,1)S(1)}, u32[]{:S(2)}, u32[]{:S(2)}) collective-permute-start(bf16[2,2,16,256]{3,2,1,0:T(8,128)(2,1)S(1)} %get-tuple-element.13), channel_id=1, source_target_pairs={{0,6},{2,14},{4,2},{6,10},{8,4},{10,12},{12,0},{14,8},{1,7},{3,15}... | collective-permute-start | bytes 98312 | tf_op jit(solution)/shard_map/ppermute | solution.py:132
  4.9 7.0 %collective-permute-start.1 = (bf16[2,2,16,256]{3,2,1,0:T(8,128)(2,1)S(1)}, bf16[2,2,16,256]{3,2,1,0:T(8,128)(2,1)S(1)}, u32[]{:S(2)}, u32[]{:S(2)}) collective-permute-start(bf16[2,2,16,256]{3,2,1,0:T(8,128)(2,1)S(1)} %get-tuple-element.14.refs_5_), channel_id=1, source_target_pairs={{0,2},{2,10},{4,6},{6,14},{8,0},{10,8},{12,4},{14,12},{1,3},{3,11}... | collective-permute-start | bytes 98312 | tf_op jit(solution)/shard_map/ppermute | solution.py:132
  6.1 7.9 %collective-permute-start = (bf16[2,2,16,256]{3,2,1,0:T(8,128)(2,1)S(1)}, bf16[2,2,16,256]{3,2,1,0:T(8,128)(2,1)S(1)}, u32[]{:S(2)}, u32[]{:S(2)}) collective-permute-start(bf16[2,2,16,256]{3,2,1,0:T(8,128)(2,1)S(1)} %get-tuple-element.14.refs_5_), channel_id=1, source_target_pairs={{2,8},{6,12},{8,2},{12,6},{3,9},{7,13},{9,3},{13,7},{18,24},{22,28... | collective-permute-start | bytes 98312 | tf_op jit(solution)/shard_map/ppermute | solution.py:132

commit v3 on v2

--- a/solution.py
+++ b/solution.py
@@ -9,20 +9,74 @@
 GROUP = ("tile", "member")
 
 
+TUNED = {
+    (4, 2): (
+        (2, 6, 3, 4, 0, 7, 1, 5),
+        (2, 5, 0, 7, 1, 6, 3, 4),
+        (1, 7, 0, 6, 3, 4, 2, 5),
+        (3, 4, 1, 5, 2, 7, 0, 6),
+    ),
+}
+
+
 def plan(n_tile, n_mem):
+    if (n_tile, n_mem) in TUNED:
+        return TUNED[n_tile, n_mem]
     per = n_tile // n_mem
     steps = []
     for k in range(per):
         for j in range(n_mem):
-            pairs = []
-            for o in range(n_tile):
-                for mm in range(n_mem):
-                    s = mm * per + (o + k) % per
-                    m = (o // per + j) % n_mem
-                    if (s, m) != (o, mm):
-                        pairs.append((o * n_mem + mm, s * n_mem + m))
-            steps.append((k, j, pairs))
-    return steps
+            to = [
+                (mm * per + (o + k) % per) * n_mem + (o // per + j) % n_mem
+                for o in range(n_tile)
+                for mm in range(n_mem)
+            ]
+            idle = [d for d, t in enumerate(to) if d == t]
+            for d, t in zip(idle, idle[1:] + idle[:1]):
+                to[d] = t
+            steps.append(tuple(to))
+    return tuple(steps)
+
+
+def serves(n_tile, n_mem, device, target):
+    per = n_tile // n_mem
+    mm, s = device % n_mem, target // n_mem
+    return s % per if s // per == mm else None
+
+
+def packed(values, width, index):
+    word = sum(v << (width * i) for i, v in enumerate(values))
+    return jnp.bitwise_and(jnp.right_shift(jnp.int32(word), index * width), (1 << width) - 1)
+
+
+def sent_block(n_tile, n_mem, step, to):
+    per = n_tile // n_mem
+    here, member = lax.axis_index("tile"), lax.axis_index("member")
+    if (n_tile, n_mem) not in TUNED:
+        return (here + step // n_mem) % per
+    width = max(1, (per - 1).bit_length())
+    sources = [serves(n_tile, n_mem, d, t) or 0 for d, t in enumerate(to)]
+    return packed(sources, width, here * n_mem + member)
+
+
+def arrival(n_tile, n_mem, owner):
+    per = n_tile // n_mem
+    here, member = lax.axis_index("tile"), lax.axis_index("member")
+    if (n_tile, n_mem) in TUNED:
+        device = here * n_mem + member
+        steps = TUNED[n_tile, n_mem]
+        width = n_tile.bit_length()
+        out = jnp.int32(0)
+        for o in range(n_tile):
+            came = []
+            for d in range(n_tile * n_mem):
+                holder = o * n_mem + d // n_mem // per
+                came.append(n_tile if holder == d else [to[holder] for to in steps].index(d))
+            out = jnp.where(owner == o, packed(came, width, device), out)
+        return out
+    k, j = (here - owner) % per, (member - owner // per) % n_mem
+    mine = jnp.logical_and(owner == here, here // per == member)
+    return jnp.where(mine, n_tile, k * n_mem + j)
 
 
 def chunk_tiles(tiles, members, rows):
@@ -86,12 +140,10 @@
 def after(sizes, ring, owners_ref, pred_ref, valid_ref, colt_ref, rowt_ref, own_ref, *refs):
     tiles, chunk, members, rows, cols = sizes
     n_tile, n_mem = ring
-    per = n_tile // n_mem
     half_r, half_c = rows // 2, cols // 2
     arrived, out_ref, scenes = refs[:n_tile], refs[n_tile], refs[n_tile + 1]
     fields = chunk * members
     fr, fh = fields * rows, fields * half_r
-    here, member = lax.axis_index("tile"), lax.axis_index("member")
     for p in range(n_tile):
         scenes[p] = arrived[p][...]
     scenes[n_tile] = own_ref[...]
@@ -102,10 +154,7 @@
             rank = 0
             for u in range(t):
                 rank = rank + jnp.where(owner[u] == owner[t], 1, 0)
-            k = (here - owner[t]) % per
-            j = (member - owner[t] // per) % n_mem
-            mine = jnp.logical_and(owner[t] == here, here // per == member)
-            step = jnp.where(mine, n_tile, k * n_mem + j)
+            step = arrival(n_tile, n_mem, owner[t])
             seen = scenes[step, 0, rank].astype(jnp.float32)
             sigma = scenes[step, 1, rank].astype(jnp.float32)
             weight = valid_ref[t * half_r : (t + 1) * half_r, :] / (sigma * sigma)
@@ -126,10 +175,12 @@
     half_r, half_c = rows // 2, cols // 2
     per = n_tile // n_mem
     both = jnp.stack([scene_lai[0, 0], scene_sigma[0, 0]], 0)
-    here = lax.axis_index("tile")
-    blocks = [lax.dynamic_slice_in_dim(both, (here + k) % per * CAP, CAP, 1) for k in range(per)]
-    own = blocks[0]
-    arrived = [lax.ppermute(blocks[k], GROUP, pairs) for k, j, pairs in plan(n_tile, n_mem)]
+    own = lax.dynamic_slice_in_dim(both, lax.axis_index("tile") % per * CAP, CAP, 1)
+    steps = plan(n_tile, n_mem)
+    arrived = []
+    for p in range(n_tile):
+        block = lax.dynamic_slice_in_dim(both, sent_block(n_tile, n_mem, p, steps[p]) * CAP, CAP, 1)
+        arrived.append(lax.ppermute(block, GROUP, list(enumerate(steps[p]))))
     arrived = [pltpu.with_memory_space_constraint(x, pltpu.VMEM) for x in arrived]
     chunk = chunk_tiles(tiles, members, rows)
     sizes = (tiles, chunk, members, rows, cols)

time: 16.1 us -> 13.4 us (0.83)
  starting transfers between devices: 8.9 us -> 6.91 us
  waiting for transfers between devices: 2.22 us -> 1.56 us
    ppermute x4, starting transfers between devices: 8.9 us -> 6.91 us  [per_device(): arrived.append(lax.ppermute(block, GROUP, list(enumerate(steps[p]))))]
    ppermute x4, waiting for transfers between devices: 2.22 us -> 1.56 us  [per_device(): arrived.append(lax.ppermute(block, GROUP, list(enumerate(steps[p]))))]
  transfers between devices with their start and end apart: 4 -> 4, of which waited for: 1 -> 2; matrix products, arithmetic and copies ran while one was open for 0% -> 0% of each run, Pallas kernels for 13% -> 16%
where the time goes in v3:
time: 13.4 us; the launch traced here: 13.2 us
  starting transfers between devices  6.91 us (52%)
  Pallas kernels  3.89 us (29%)
  waiting for transfers between devices  1.56 us (12%)
  local copies, waits for them, and re-layouts  0.77 us (6%)
    ppermute x4, starting transfers between devices, per_device(): arrived.append(lax.ppermute(block, GROUP, list(enumerate(steps[p]))))  6.91 us
    pallas_call x1, Pallas kernels, per_device(): pl.pallas_call(lambda *refs: before(sizes, *refs), out_shape=(pltpu.VMEM(...  2.13 us
    pallas_call x1, Pallas kernels, per_device(): pl.pallas_call(lambda *refs: after(sizes, (n_tile, n_mem), *refs), out_sh...  1.77 us
    ppermute x4, waiting for transfers between devices, per_device(): arrived.append(lax.ppermute(block, GROUP, list(enumerate(steps[p]))))  1.56 us
    unnamed x4, local copies, waits for them, and re-layouts  0.77 us
  transfers between devices with their start and end apart: 4, of which 2 were waited for; matrix products, arithmetic and copies ran while one was open for 0% of the time, Pallas kernels for 16%

profile of v3, /device:TPU:2, one launch (start us, length us, event | category | flops | bytes accessed | tf_op | source)
XLA Modules:
  0.0 13.2 jit_solution(18319020039348011878)
XLA Ops:
  0.0 0.0 copy-start.1
  0.0 0.0 copy-start
  0.0 0.8 %copy-done.1 = bf16[1,1,4,16,256]{4,3,2,1,0:T(8,128)(2,1)S(1)} copy-done((bf16[1,1,4,16,256]{4,3,2,1,0:T(8,128)(2,1)S(1)}, bf16[1,1,4,16,256]{4,3,2,1,0:T(8,128)(2,1)}, u32[]{:S(2)}) %copy-start.1) | copy-done | bytes 32792
  0.8 0.0 copy-done
  0.8 2.6 %collective-permute-start.3 = (bf16[2,2,16,256]{3,2,1,0:T(8,128)(2,1)S(1)}, bf16[2,2,16,256]{3,2,1,0:T(8,128)(2,1)S(1)}, u32[]{:S(2)}, u32[]{:S(2)}) collective-permute-start(bf16[2,2,16,256]{3,2,1,0:T(8,128)(2,1)S(1)} %get-tuple-element.13), channel_id=1, source_target_pairs={{0,6},{2,8},{4,2},{6,10},{8,4},{10,14},{12,0},{14,12},{1,7},{3,9},... | collective-permute-start | bytes 98312 | tf_op jit(solution)/shard_map/ppermute | solution.py:183
  3.4 1.1 %collective-permute-start = (bf16[2,2,16,256]{3,2,1,0:T(8,128)(2,1)S(1)}, bf16[2,2,16,256]{3,2,1,0:T(8,128)(2,1)S(1)}, u32[]{:S(2)}, u32[]{:S(2)}) collective-permute-start(bf16[2,2,16,256]{3,2,1,0:T(8,128)(2,1)S(1)} %get-tuple-element.15), channel_id=1, source_target_pairs={{0,4},{2,12},{4,6},{6,8},{8,0},{10,14},{12,2},{14,10},{1,5},{3,13}... | collective-permute-start | bytes 98312 | tf_op jit(solution)/shard_map/ppermute | solution.py:183
  4.5 1.1 %collective-permute-start.1 = (bf16[2,2,16,256]{3,2,1,0:T(8,128)(2,1)S(1)}, bf16[2,2,16,256]{3,2,1,0:T(8,128)(2,1)S(1)}, u32[]{:S(2)}, u32[]{:S(2)}) collective-permute-start(bf16[2,2,16,256]{3,2,1,0:T(8,128)(2,1)S(1)} %get-tuple-element.16), channel_id=1, source_target_pairs={{0,4},{2,10},{4,0},{6,14},{8,2},{10,12},{12,6},{14,8},{1,5},{3,11}... | collective-permute-start | bytes 98312 | tf_op jit(solution)/shard_map/ppermute | solution.py:183
  5.5 2.2 %collective-permute-start.2 = (bf16[2,2,16,256]{3,2,1,0:T(8,128)(2,1)S(1)}, bf16[2,2,16,256]{3,2,1,0:T(8,128)(2,1)S(1)}, u32[]{:S(2)}, u32[]{:S(2)}) collective-permute-start(bf16[2,2,16,256]{3,2,1,0:T(8,128)(2,1)S(1)} %get-tuple-element.17), channel_id=1, source_target_pairs={{0,2},{2,14},{4,0},{6,12},{8,6},{10,8},{12,4},{14,10},{1,3},{3,15}... | collective-permute-start | bytes 98312 | tf_op jit(solution)/shard_map/ppermute | solution.py:183
  7.7 2.1 %before.1 = (bf16[128,256]{1,0:T(8,128)(2,1)S(1)}, f32[64,256]{1,0:T(8,128)S(1)}, bf16[256,512]{1,0:T(8,128)(2,1)S(1)}, bf16[256,128]{1,0:T(8,128)(2,1)S(1)}) custom-call(f32[2,7]{1,0:T(2,128)} %refs_0_.2, s32[4,32]{1,0:T(4,128)} %bitcast.8, bf16[256,512]{1,0:T(8,128)(2,1)} %bitcast.5), custom_call_target="tpu_custom_call" | custom-call | tf_op jit(solution)/shard_map/before/pallas_call | solution.py:191
  9.8 0.0 collective-permute-done.3.refs_9_
  9.9 0.2 %collective-permute-done.refs_6_ = bf16[2,2,16,256]{3,2,1,0:T(8,128)(2,1)S(1)} collective-permute-done((bf16[2,2,16,256]{3,2,1,0:T(8,128)(2,1)S(1)}, bf16[2,2,16,256]{3,2,1,0:T(8,128)(2,1)S(1)}, u32[]{:S(2)}, u32[]{:S(2)}) %collective-permute-start) | collective-permute-done | bytes 32800 | tf_op jit(solution)/shard_map/ppermute | solution.py:183
  10.1 1.3 %collective-permute-done.1.refs_7_ = bf16[2,2,16,256]{3,2,1,0:T(8,128)(2,1)S(1)} collective-permute-done((bf16[2,2,16,256]{3,2,1,0:T(8,128)(2,1)S(1)}, bf16[2,2,16,256]{3,2,1,0:T(8,128)(2,1)S(1)}, u32[]{:S(2)}, u32[]{:S(2)}) %collective-permute-start.1) | collective-permute-done | bytes 32800 | tf_op jit(solution)/shard_map/ppermute | solution.py:183
  11.4 0.0 collective-permute-done.2.refs_8_
  11.4 1.8 %after.1 = bf16[256,512]{1,0:T(8,128)(2,1)} custom-call(s32[1,4]{1,0:T(1,128)} %refs_0_.3, bf16[128,256]{1,0:T(8,128)(2,1)S(1)} %get-tuple-element.9.refs_1_, f32[64,256]{1,0:T(8,128)S(1)} %get-tuple-element.10.refs_2_, bf16[256,512]{1,0:T(8,128)(2,1)S(1)} %get-tuple-element.11.refs_3_, bf16[256,128]{1,0:T(8,128)(2,1)S(1)} %get-tuple-element.12.refs_4_, ...), custom_call_target="tpu_custom_call" | custom-call | tf_op jit(solution)/shard_map/after/pallas_call | solution.py:205
  (1 shorter events, 0.0 us)
Async XLA Ops:
  0.0 0.8 %copy-start.1 = (bf16[1,1,4,16,256]{4,3,2,1,0:T(8,128)(2,1)S(1)}, bf16[1,1,4,16,256]{4,3,2,1,0:T(8,128)(2,1)}, u32[]{:S(2)}) copy-start(bf16[1,1,4,16,256]{4,3,2,1,0:T(8,128)(2,1)} %param.10) | copy-start | bytes 98308
  0.0 0.8 %copy-start = (bf16[1,1,4,16,256]{4,3,2,1,0:T(8,128)(2,1)S(1)}, bf16[1,1,4,16,256]{4,3,2,1,0:T(8,128)(2,1)}, u32[]{:S(2)}) copy-start(bf16[1,1,4,16,256]{4,3,2,1,0:T(8,128)(2,1)} %param.9) | copy-start | bytes 98308
  0.8 9.1 %collective-permute-start.3 = (bf16[2,2,16,256]{3,2,1,0:T(8,128)(2,1)S(1)}, bf16[2,2,16,256]{3,2,1,0:T(8,128)(2,1)S(1)}, u32[]{:S(2)}, u32[]{:S(2)}) collective-permute-start(bf16[2,2,16,256]{3,2,1,0:T(8,128)(2,1)S(1)} %get-tuple-element.13), channel_id=1, source_target_pairs={{0,6},{2,8},{4,2},{6,10},{8,4},{10,14},{12,0},{14,12},{1,7},{3,9},... | collective-permute-start | bytes 98312 | tf_op jit(solution)/shard_map/ppermute | solution.py:183
  3.4 6.7 %collective-permute-start = (bf16[2,2,16,256]{3,2,1,0:T(8,128)(2,1)S(1)}, bf16[2,2,16,256]{3,2,1,0:T(8,128)(2,1)S(1)}, u32[]{:S(2)}, u32[]{:S(2)}) collective-permute-start(bf16[2,2,16,256]{3,2,1,0:T(8,128)(2,1)S(1)} %get-tuple-element.15), channel_id=1, source_target_pairs={{0,4},{2,12},{4,6},{6,8},{8,0},{10,14},{12,2},{14,10},{1,5},{3,13}... | collective-permute-start | bytes 98312 | tf_op jit(solution)/shard_map/ppermute | solution.py:183
  4.5 6.9 %collective-permute-start.1 = (bf16[2,2,16,256]{3,2,1,0:T(8,128)(2,1)S(1)}, bf16[2,2,16,256]{3,2,1,0:T(8,128)(2,1)S(1)}, u32[]{:S(2)}, u32[]{:S(2)}) collective-permute-start(bf16[2,2,16,256]{3,2,1,0:T(8,128)(2,1)S(1)} %get-tuple-element.16), channel_id=1, source_target_pairs={{0,4},{2,10},{4,0},{6,14},{8,2},{10,12},{12,6},{14,8},{1,5},{3,11}... | collective-permute-start | bytes 98312 | tf_op jit(solution)/shard_map/ppermute | solution.py:183
  5.5 5.9 %collective-permute-start.2 = (bf16[2,2,16,256]{3,2,1,0:T(8,128)(2,1)S(1)}, bf16[2,2,16,256]{3,2,1,0:T(8,128)(2,1)S(1)}, u32[]{:S(2)}, u32[]{:S(2)}) collective-permute-start(bf16[2,2,16,256]{3,2,1,0:T(8,128)(2,1)S(1)} %get-tuple-element.17), channel_id=1, source_target_pairs={{0,2},{2,14},{4,0},{6,12},{8,6},{10,8},{12,4},{14,10},{1,3},{3,15}... | collective-permute-start | bytes 98312 | tf_op jit(solution)/shard_map/ppermute | solution.py:183

commit v4 on v3

--- a/solution.py
+++ b/solution.py
@@ -6,15 +6,16 @@
 from jax.sharding import PartitionSpec as P
 
 CAP = 2
+PIECES = 2
 GROUP = ("tile", "member")
 
 
 TUNED = {
     (4, 2): (
-        (2, 6, 3, 4, 0, 7, 1, 5),
-        (2, 5, 0, 7, 1, 6, 3, 4),
-        (1, 7, 0, 6, 3, 4, 2, 5),
-        (3, 4, 1, 5, 2, 7, 0, 6),
+        (3, 6, 1, 7, 0, 4, 2, 5),
+        (5, 4, 0, 6, 3, 7, 1, 2),
+        (2, 7, 0, 5, 1, 6, 3, 4),
+        (1, 5, 3, 4, 2, 7, 0, 6),
     ),
 }
 
@@ -98,10 +99,16 @@
     return out.astype(jnp.bfloat16)
 
 
-def before(sizes, taps_ref, words_ref, field_ref, pred_ref, valid_ref, colt_ref, rowt_ref, pad):
+def before(sizes, ring, owners_ref, taps_ref, words_ref, field_ref, pred_ref, valid_ref, colt_ref, rowt_ref, pick_ref, pad):
     tiles, chunk, members, rows, cols = sizes
     half_r, half_c = rows // 2, cols // 2
     n_words = words_ref.shape[1]
+    owner = [owners_ref[0, t] for t in range(tiles)]
+    for t in range(tiles):
+        rank = 0
+        for u in range(t):
+            rank = rank + jnp.where(owner[u] == owner[t], 1, 0)
+        pick_ref[t] = arrival(*ring, owner[t]) * CAP + rank
     taps = taps_ref[...]
     taps = taps / jnp.sum(taps, axis=1, keepdims=True)
     reach = taps.shape[1] // 2
@@ -137,26 +144,24 @@
                 valid_ref[t * half_r + i0 : t * half_r + i0 + 8, j0 : j0 + 128] = bit.astype(jnp.float32)
 
 
-def after(sizes, ring, owners_ref, pred_ref, valid_ref, colt_ref, rowt_ref, own_ref, *refs):
+def after(sizes, n_tile, pick_ref, pred_ref, valid_ref, colt_ref, rowt_ref, own_ref, *refs):
     tiles, chunk, members, rows, cols = sizes
-    n_tile, n_mem = ring
     half_r, half_c = rows // 2, cols // 2
-    arrived, out_ref, scenes = refs[:n_tile], refs[n_tile], refs[n_tile + 1]
+    arrived, out_ref, scenes, update, sems = refs[:n_tile], refs[n_tile], *refs[n_tile + 1 :]
     fields = chunk * members
     fr, fh = fields * rows, fields * half_r
-    for p in range(n_tile):
-        scenes[p] = arrived[p][...]
-    scenes[n_tile] = own_ref[...]
-    owner = [owners_ref[0, t] for t in range(tiles)]
+    for p, block in enumerate((*arrived, own_ref)):
+        for r in range(CAP):
+            for kind in range(2):
+                scenes[p * CAP + r, kind] = block[kind, r]
+    cuts = PIECES if fields % PIECES == 0 else 1
+    pr, ph = fr // cuts, fh // cuts
+    copies = []
     for g in range(tiles // chunk):
         parts = []
         for t in range(g * chunk, (g + 1) * chunk):
-            rank = 0
-            for u in range(t):
-                rank = rank + jnp.where(owner[u] == owner[t], 1, 0)
-            step = arrival(n_tile, n_mem, owner[t])
-            seen = scenes[step, 0, rank].astype(jnp.float32)
-            sigma = scenes[step, 1, rank].astype(jnp.float32)
+            seen = scenes[pick_ref[t], 0].astype(jnp.float32)
+            sigma = scenes[pick_ref[t], 1].astype(jnp.float32)
             weight = valid_ref[t * half_r : (t + 1) * half_r, :] / (sigma * sigma)
             for m in range(members):
                 at = (t * members + m) * half_r
@@ -164,9 +169,15 @@
                 parts.append((gap * weight).astype(jnp.bfloat16))
         misfit = jnp.concatenate(parts, axis=0)
         spread = jnp.dot(misfit, colt_ref[...], preferred_element_type=jnp.float32).astype(jnp.bfloat16)
-        out_ref[g * fr : (g + 1) * fr, :] = jnp.dot(
-            rowt_ref[...], spread, preferred_element_type=jnp.float32
-        ).astype(jnp.bfloat16)
+        for c in range(cuts):
+            at = pl.ds(g * fr + c * pr, pr)
+            update[at, :] = jnp.dot(
+                rowt_ref[:pr, :ph], spread[c * ph : (c + 1) * ph, :], preferred_element_type=jnp.float32
+            ).astype(jnp.bfloat16)
+            copies.append(pltpu.make_async_copy(update.at[at, :], out_ref.at[at, :], sems.at[len(copies)]))
+            copies[-1].start()
+    for copy in copies:
+        copy.wait()
 
 
 def per_device(sim_lai, owner_ids, cloud_words, scene_lai, scene_sigma, mtf_taps):
@@ -188,28 +199,34 @@
     fr, fh = fields * rows, fields * half_r
     vmem = pl.BlockSpec(memory_space=pltpu.VMEM)
     smem = pl.BlockSpec(memory_space=pltpu.SMEM)
-    pred, valid, colt, rowt = pl.pallas_call(
-        lambda *refs: before(sizes, *refs),
+    pred, valid, colt, rowt, picks = pl.pallas_call(
+        lambda *refs: before(sizes, (n_tile, n_mem), *refs),
         out_shape=(
             pltpu.VMEM((tiles * members * half_r, half_c), jnp.bfloat16),
             pltpu.VMEM((tiles * half_r, half_c), jnp.float32),
             pltpu.VMEM((half_c, cols), jnp.bfloat16),
             pltpu.VMEM((fr, fh), jnp.bfloat16),
+            pltpu.SMEM((tiles,), jnp.int32),
         ),
-        in_specs=[vmem] * 3,
-        out_specs=[vmem] * 4,
+        in_specs=[smem] + [vmem] * 3,
+        out_specs=[vmem] * 4 + [smem],
         scratch_shapes=[pltpu.VMEM((tiles, 128), jnp.int32)],
         name="before",
-    )(mtf_taps, cloud_words[0], sim_lai.reshape(tiles * members * rows, cols))
+    )(owner_ids, mtf_taps, cloud_words[0], sim_lai.reshape(tiles * members * rows, cols))
     resident = [pltpu.with_memory_space_constraint(x, pltpu.VMEM) for x in (pred, valid, colt, rowt, own)]
+    picks = pltpu.with_memory_space_constraint(picks, pltpu.SMEM)
     out = pl.pallas_call(
-        lambda *refs: after(sizes, (n_tile, n_mem), *refs),
+        lambda *refs: after(sizes, n_tile, *refs),
         out_shape=jax.ShapeDtypeStruct((tiles * members * rows, cols), jnp.bfloat16),
         in_specs=[smem] + [vmem] * (5 + n_tile),
-        out_specs=vmem,
-        scratch_shapes=[pltpu.VMEM((n_tile + 1, 2, CAP, half_r, half_c), jnp.bfloat16)],
+        out_specs=pl.BlockSpec(memory_space=pl.ANY),
+        scratch_shapes=[
+            pltpu.VMEM(((n_tile + 1) * CAP, 2, half_r, half_c), jnp.bfloat16),
+            pltpu.VMEM((tiles * members * rows, cols), jnp.bfloat16),
+            pltpu.SemaphoreType.DMA((PIECES * tiles // chunk,)),
+        ],
         name="after",
-    )(owner_ids, *resident, *arrived)
+    )(picks, *resident, *arrived)
     return out.reshape(sim_lai.shape)
 
 

time: 13.4 us -> 12.8 us (0.955)
  the two profiles are of different devices: /device:TPU:2 before, /device:TPU:0 now
where the time goes in v4:
time: 12.8 us; the launch traced here: 12.6 us
  starting transfers between devices  7.58 us (59%)
  Pallas kernels  3.19 us (25%)
  waiting for transfers between devices  0.97 us (8%)
  local copies, waits for them, and re-layouts  0.77 us (6%)
    ppermute x4, starting transfers between devices, per_device(): arrived.append(lax.ppermute(block, GROUP, list(enumerate(steps[p]))))  7.58 us
    pallas_call x1, Pallas kernels, per_device(): pl.pallas_call(lambda *refs: before(sizes, (n_tile, n_mem), *refs), out_s...  2.14 us
    pallas_call x1, Pallas kernels, per_device(): pl.pallas_call(lambda *refs: after(sizes, n_tile, *refs), out_shape=jax.S...  1.05 us
    ppermute x4, waiting for transfers between devices, per_device(): arrived.append(lax.ppermute(block, GROUP, list(enumerate(steps[p]))))  0.97 us
    unnamed x4, local copies, waits for them, and re-layouts  0.77 us
  transfers between devices with their start and end apart: 4, of which 2 were waited for; matrix products, arithmetic and copies ran while one was open for 0% of the time, Pallas kernels for 17%

profile of v4, /device:TPU:0, one launch (start us, length us, event | category | flops | bytes accessed | tf_op | source)
XLA Modules:
  0.0 12.6 jit_solution(15081022664284517355)
XLA Ops:
  0.0 0.0 copy-start.1
  0.0 0.0 copy-start
  0.0 0.8 %copy-done.1 = bf16[1,1,4,16,256]{4,3,2,1,0:T(8,128)(2,1)S(1)} copy-done((bf16[1,1,4,16,256]{4,3,2,1,0:T(8,128)(2,1)S(1)}, bf16[1,1,4,16,256]{4,3,2,1,0:T(8,128)(2,1)}, u32[]{:S(2)}) %copy-start.1) | copy-done | bytes 32792
  0.8 0.0 copy-done
  0.8 3.0 %collective-permute-start.3 = (bf16[2,2,16,256]{3,2,1,0:T(8,128)(2,1)S(1)}, bf16[2,2,16,256]{3,2,1,0:T(8,128)(2,1)S(1)}, u32[]{:S(2)}, u32[]{:S(2)}) collective-permute-start(bf16[2,2,16,256]{3,2,1,0:T(8,128)(2,1)S(1)} %get-tuple-element.15), channel_id=1, source_target_pairs={{0,2},{2,10},{4,6},{6,8},{8,4},{10,14},{12,0},{14,12},{1,3},{3,11}... | collective-permute-start | bytes 98312 | tf_op jit(solution)/shard_map/ppermute | solution.py:194
  3.8 2.6 %collective-permute-start = (bf16[2,2,16,256]{3,2,1,0:T(8,128)(2,1)S(1)}, bf16[2,2,16,256]{3,2,1,0:T(8,128)(2,1)S(1)}, u32[]{:S(2)}, u32[]{:S(2)}) collective-permute-start(bf16[2,2,16,256]{3,2,1,0:T(8,128)(2,1)S(1)} %get-tuple-element.17), channel_id=1, source_target_pairs={{0,6},{2,12},{4,2},{6,14},{8,0},{10,8},{12,4},{14,10},{1,7},{3,13}... | collective-permute-start | bytes 98312 | tf_op jit(solution)/shard_map/ppermute | solution.py:194
  6.3 1.0 %collective-permute-start.1 = (bf16[2,2,16,256]{3,2,1,0:T(8,128)(2,1)S(1)}, bf16[2,2,16,256]{3,2,1,0:T(8,128)(2,1)S(1)}, u32[]{:S(2)}, u32[]{:S(2)}) collective-permute-start(bf16[2,2,16,256]{3,2,1,0:T(8,128)(2,1)S(1)} %get-tuple-element.18), channel_id=1, source_target_pairs={{0,10},{2,8},{4,0},{6,12},{8,6},{10,14},{12,2},{14,4},{1,11},{3,9}... | collective-permute-start | bytes 98312 | tf_op jit(solution)/shard_map/ppermute | solution.py:194
  7.4 1.0 %collective-permute-start.2 = (bf16[2,2,16,256]{3,2,1,0:T(8,128)(2,1)S(1)}, bf16[2,2,16,256]{3,2,1,0:T(8,128)(2,1)S(1)}, u32[]{:S(2)}, u32[]{:S(2)}) collective-permute-start(bf16[2,2,16,256]{3,2,1,0:T(8,128)(2,1)S(1)} %get-tuple-element.19), channel_id=1, source_target_pairs={{0,4},{2,14},{4,0},{6,10},{8,2},{10,12},{12,6},{14,8},{1,5},{3,15}... | collective-permute-start | bytes 98312 | tf_op jit(solution)/shard_map/ppermute | solution.py:194
  8.4 2.1 %before.1 = (bf16[128,256]{1,0:T(8,128)(2,1)S(1)}, f32[64,256]{1,0:T(8,128)S(1)}, bf16[256,512]{1,0:T(8,128)(2,1)S(1)}, bf16[256,128]{1,0:T(8,128)(2,1)S(1)}, s32[4]{0:T(128)S(4)}) custom-call(s32[1,4]{1,0:T(1,128)} %refs_0_.1, f32[2,7]{1,0:T(2,128)} %refs_1_.1, s32[4,32]{1,0:T(4,128)} %bitcast.8, bf16[256,512]{1,0:T(8,128)(2,1)} %bitcast.5), custom_call_target="tpu_custom_call" | custom-call | tf_op jit(solution)/shard_map/before/pallas_call | solution.py:202
  10.5 0.0 collective-permute-done.3.refs_9_
  10.5 0.0 collective-permute-done.refs_6_
  10.5 0.1 collective-permute-done.1.refs_7_
  10.7 0.8 %collective-permute-done.2.refs_8_ = bf16[2,2,16,256]{3,2,1,0:T(8,128)(2,1)S(1)} collective-permute-done((bf16[2,2,16,256]{3,2,1,0:T(8,128)(2,1)S(1)}, bf16[2,2,16,256]{3,2,1,0:T(8,128)(2,1)S(1)}, u32[]{:S(2)}, u32[]{:S(2)}) %collective-permute-start.2) | collective-permute-done | bytes 32800 | tf_op jit(solution)/shard_map/ppermute | solution.py:194
  11.5 1.1 %after.1 = bf16[256,512]{1,0:T(8,128)(2,1)} custom-call(s32[4]{0:T(128)S(4)} %get-tuple-element.10.refs_0_, bf16[128,256]{1,0:T(8,128)(2,1)S(1)} %get-tuple-element.11.refs_1_, f32[64,256]{1,0:T(8,128)S(1)} %get-tuple-element.12.refs_2_, bf16[256,512]{1,0:T(8,128)(2,1)S(1)} %get-tuple-element.13.refs_3_, bf16[256,128]{1,0:T(8,128)(2,1)S(1)} %get-tuple-element.14.refs_4_, ...), custom_call_target="tpu_custom_call" | custom-call | tf_op jit(solution)/shard_map/after/pallas_call | solution.py:218
  (1 shorter events, 0.0 us)
Async XLA Ops:
  0.0 0.8 %copy-start.1 = (bf16[1,1,4,16,256]{4,3,2,1,0:T(8,128)(2,1)S(1)}, bf16[1,1,4,16,256]{4,3,2,1,0:T(8,128)(2,1)}, u32[]{:S(2)}) copy-start(bf16[1,1,4,16,256]{4,3,2,1,0:T(8,128)(2,1)} %param.10) | copy-start | bytes 98308
  0.0 0.8 %copy-start = (bf16[1,1,4,16,256]{4,3,2,1,0:T(8,128)(2,1)S(1)}, bf16[1,1,4,16,256]{4,3,2,1,0:T(8,128)(2,1)}, u32[]{:S(2)}) copy-start(bf16[1,1,4,16,256]{4,3,2,1,0:T(8,128)(2,1)} %param.9) | copy-start | bytes 98308
  0.8 9.7 %collective-permute-start.3 = (bf16[2,2,16,256]{3,2,1,0:T(8,128)(2,1)S(1)}, bf16[2,2,16,256]{3,2,1,0:T(8,128)(2,1)S(1)}, u32[]{:S(2)}, u32[]{:S(2)}) collective-permute-start(bf16[2,2,16,256]{3,2,1,0:T(8,128)(2,1)S(1)} %get-tuple-element.15), channel_id=1, source_target_pairs={{0,2},{2,10},{4,6},{6,8},{8,4},{10,14},{12,0},{14,12},{1,3},{3,11}... | collective-permute-start | bytes 98312 | tf_op jit(solution)/shard_map/ppermute | solution.py:194
  3.8 6.7 %collective-permute-start = (bf16[2,2,16,256]{3,2,1,0:T(8,128)(2,1)S(1)}, bf16[2,2,16,256]{3,2,1,0:T(8,128)(2,1)S(1)}, u32[]{:S(2)}, u32[]{:S(2)}) collective-permute-start(bf16[2,2,16,256]{3,2,1,0:T(8,128)(2,1)S(1)} %get-tuple-element.17), channel_id=1, source_target_pairs={{0,6},{2,12},{4,2},{6,14},{8,0},{10,8},{12,4},{14,10},{1,7},{3,13}... | collective-permute-start | bytes 98312 | tf_op jit(solution)/shard_map/ppermute | solution.py:194
  6.3 4.3 %collective-permute-start.1 = (bf16[2,2,16,256]{3,2,1,0:T(8,128)(2,1)S(1)}, bf16[2,2,16,256]{3,2,1,0:T(8,128)(2,1)S(1)}, u32[]{:S(2)}, u32[]{:S(2)}) collective-permute-start(bf16[2,2,16,256]{3,2,1,0:T(8,128)(2,1)S(1)} %get-tuple-element.18), channel_id=1, source_target_pairs={{0,10},{2,8},{4,0},{6,12},{8,6},{10,14},{12,2},{14,4},{1,11},{3,9}... | collective-permute-start | bytes 98312 | tf_op jit(solution)/shard_map/ppermute | solution.py:194
  7.4 4.1 %collective-permute-start.2 = (bf16[2,2,16,256]{3,2,1,0:T(8,128)(2,1)S(1)}, bf16[2,2,16,256]{3,2,1,0:T(8,128)(2,1)S(1)}, u32[]{:S(2)}, u32[]{:S(2)}) collective-permute-start(bf16[2,2,16,256]{3,2,1,0:T(8,128)(2,1)S(1)} %get-tuple-element.19), channel_id=1, source_target_pairs={{0,4},{2,14},{4,0},{6,10},{8,2},{10,12},{12,6},{14,8},{1,5},{3,15}... | collective-permute-start | bytes 98312 | tf_op jit(solution)/shard_map/ppermute | solution.py:194

commit v5 on v4

--- a/solution.py
+++ b/solution.py
@@ -7,15 +7,15 @@
 
 CAP = 2
 PIECES = 2
-GROUP = ("tile", "member")
+GROUP = ("tile", "member", "date")
 
 
 TUNED = {
     (4, 2): (
-        (3, 6, 1, 7, 0, 4, 2, 5),
-        (5, 4, 0, 6, 3, 7, 1, 2),
-        (2, 7, 0, 5, 1, 6, 3, 4),
-        (1, 5, 3, 4, 2, 7, 0, 6),
+        (1, 5, 3, 6, 0, 4, 2, 7),
+        (2, 6, 0, 5, 3, 7, 1, 4),
+        (0, 7, 1, 4, 2, 6, 3, 5),
+        (3, 4, 2, 7, 1, 5, 0, 6),
     ),
 }
 
@@ -32,17 +32,16 @@
                 for o in range(n_tile)
                 for mm in range(n_mem)
             ]
-            idle = [d for d, t in enumerate(to) if d == t]
-            for d, t in zip(idle, idle[1:] + idle[:1]):
-                to[d] = t
             steps.append(tuple(to))
     return tuple(steps)
 
 
-def serves(n_tile, n_mem, device, target):
-    per = n_tile // n_mem
-    mm, s = device % n_mem, target // n_mem
-    return s % per if s // per == mm else None
+def pairs(to, n_date):
+    return [
+        (src * n_date + d, dst * n_date + (d if src != dst else (d + 1) % n_date))
+        for src, dst in enumerate(to)
+        for d in range(n_date)
+    ]
 
 
 def packed(values, width, index):
@@ -56,7 +55,7 @@
     if (n_tile, n_mem) not in TUNED:
         return (here + step // n_mem) % per
     width = max(1, (per - 1).bit_length())
-    sources = [serves(n_tile, n_mem, d, t) or 0 for d, t in enumerate(to)]
+    sources = [t // n_mem % per for t in to]
     return packed(sources, width, here * n_mem + member)
 
 
@@ -191,7 +190,7 @@
     arrived = []
     for p in range(n_tile):
         block = lax.dynamic_slice_in_dim(both, sent_block(n_tile, n_mem, p, steps[p]) * CAP, CAP, 1)
-        arrived.append(lax.ppermute(block, GROUP, list(enumerate(steps[p]))))
+        arrived.append(lax.ppermute(block, GROUP, pairs(steps[p], lax.axis_size("date"))))
     arrived = [pltpu.with_memory_space_constraint(x, pltpu.VMEM) for x in arrived]
     chunk = chunk_tiles(tiles, members, rows)
     sizes = (tiles, chunk, members, rows, cols)

time: 12.8 us -> 11.9 us (0.930)
  waiting for transfers between devices: 0.97 us -> 0.54 us
  starting transfers between devices: 7.58 us -> 7.15 us
    ppermute x4, waiting for transfers between devices: 0.97 us -> 0.54 us  [per_device(): lax.ppermute(block, GROUP, pairs(steps[p], lax.axis_size('date')))]
    ppermute x4, starting transfers between devices: 7.58 us -> 7.15 us  [per_device(): lax.ppermute(block, GROUP, pairs(steps[p], lax.axis_size('date')))]
  transfers between devices with their start and end apart: 4 -> 4, of which waited for: 2 -> 1; matrix products, arithmetic and copies ran while one was open for 0% -> 0% of each run, Pallas kernels for 17% -> 18%
where the time goes in v5:
time: 11.9 us; the launch traced here: 11.7 us
  starting transfers between devices  7.15 us (60%)
  Pallas kernels  3.2 us (27%)
  local copies, waits for them, and re-layouts  0.77 us (6%)
  waiting for transfers between devices  0.54 us (5%)
    ppermute x4, starting transfers between devices, per_device(): lax.ppermute(block, GROUP, pairs(steps[p], lax.axis_size('date')))  7.15 us
    pallas_call x1, Pallas kernels, per_device(): pl.pallas_call(lambda *refs: before(sizes, (n_tile, n_mem), *refs), out_s...  2.14 us
    pallas_call x1, Pallas kernels, per_device(): pl.pallas_call(lambda *refs: after(sizes, n_tile, *refs), out_shape=jax.S...  1.05 us
    unnamed x4, local copies, waits for them, and re-layouts  0.77 us
    ppermute x4, waiting for transfers between devices, per_device(): lax.ppermute(block, GROUP, pairs(steps[p], lax.axis_size('date')))  0.54 us
  transfers between devices with their start and end apart: 4, of which 1 were waited for; matrix products, arithmetic and copies ran while one was open for 0% of the time, Pallas kernels for 18%

profile of v5, /device:TPU:0, one launch (start us, length us, event | category | flops | bytes accessed | tf_op | source)
XLA Modules:
  0.0 11.7 jit_solution(2283681243856842974)
XLA Ops:
  0.0 0.0 copy-start.1
  0.0 0.0 copy-start
  0.0 0.8 %copy-done.1 = bf16[1,1,4,16,256]{4,3,2,1,0:T(8,128)(2,1)S(1)} copy-done((bf16[1,1,4,16,256]{4,3,2,1,0:T(8,128)(2,1)S(1)}, bf16[1,1,4,16,256]{4,3,2,1,0:T(8,128)(2,1)}, u32[]{:S(2)}) %copy-start.1) | copy-done | bytes 32792
  0.8 0.0 copy-done
  0.8 4.0 %collective-permute-start.3 = (bf16[2,2,16,256]{3,2,1,0:T(8,128)(2,1)S(1)}, bf16[2,2,16,256]{3,2,1,0:T(8,128)(2,1)S(1)}, u32[]{:S(2)}, u32[]{:S(2)}) collective-permute-start(bf16[2,2,16,256]{3,2,1,0:T(8,128)(2,1)S(1)} %get-tuple-element.15), channel_id=1, source_target_pairs={{0,6},{1,7},{2,8},{3,9},{4,5},{5,4},{6,14},{7,15},{8,2},{9,3},{10,... | collective-permute-start | bytes 98312 | tf_op jit(solution)/shard_map/ppermute | solution.py:193
  4.8 1.5 %collective-permute-start = (bf16[2,2,16,256]{3,2,1,0:T(8,128)(2,1)S(1)}, bf16[2,2,16,256]{3,2,1,0:T(8,128)(2,1)S(1)}, u32[]{:S(2)}, u32[]{:S(2)}) collective-permute-start(bf16[2,2,16,256]{3,2,1,0:T(8,128)(2,1)S(1)} %get-tuple-element.17), channel_id=1, source_target_pairs={{0,2},{1,3},{2,10},{3,11},{4,6},{5,7},{6,12},{7,13},{8,0},{9,1},{1... | collective-permute-start | bytes 98312 | tf_op jit(solution)/shard_map/ppermute | solution.py:193
  6.3 1.6 %collective-permute-start.1 = (bf16[2,2,16,256]{3,2,1,0:T(8,128)(2,1)S(1)}, bf16[2,2,16,256]{3,2,1,0:T(8,128)(2,1)S(1)}, u32[]{:S(2)}, u32[]{:S(2)}) collective-permute-start(bf16[2,2,16,256]{3,2,1,0:T(8,128)(2,1)S(1)} %get-tuple-element.18), channel_id=1, source_target_pairs={{0,4},{1,5},{2,12},{3,13},{4,0},{5,1},{6,10},{7,11},{8,6},{9,7},{1... | collective-permute-start | bytes 98312 | tf_op jit(solution)/shard_map/ppermute | solution.py:193
  7.9 0.0 collective-permute-start.2
  7.9 2.1 %before.1 = (bf16[128,256]{1,0:T(8,128)(2,1)S(1)}, f32[64,256]{1,0:T(8,128)S(1)}, bf16[256,512]{1,0:T(8,128)(2,1)S(1)}, bf16[256,128]{1,0:T(8,128)(2,1)S(1)}, s32[4]{0:T(128)S(4)}) custom-call(s32[1,4]{1,0:T(1,128)} %refs_0_.1, f32[2,7]{1,0:T(2,128)} %refs_1_.1, s32[4,32]{1,0:T(4,128)} %bitcast.8, bf16[256,512]{1,0:T(8,128)(2,1)} %bitcast.5), custom_call_target="tpu_custom_call" | custom-call | tf_op jit(solution)/shard_map/before/pallas_call | solution.py:201
  10.1 0.0 collective-permute-done.3.refs_9_
  10.1 0.0 collective-permute-done.refs_6_
  10.1 0.5 %collective-permute-done.1.refs_7_ = bf16[2,2,16,256]{3,2,1,0:T(8,128)(2,1)S(1)} collective-permute-done((bf16[2,2,16,256]{3,2,1,0:T(8,128)(2,1)S(1)}, bf16[2,2,16,256]{3,2,1,0:T(8,128)(2,1)S(1)}, u32[]{:S(2)}, u32[]{:S(2)}) %collective-permute-start.1) | collective-permute-done | bytes 32800 | tf_op jit(solution)/shard_map/ppermute | solution.py:193
  10.7 0.0 collective-permute-done.2.refs_8_
  10.7 1.1 %after.1 = bf16[256,512]{1,0:T(8,128)(2,1)} custom-call(s32[4]{0:T(128)S(4)} %get-tuple-element.10.refs_0_, bf16[128,256]{1,0:T(8,128)(2,1)S(1)} %get-tuple-element.11.refs_1_, f32[64,256]{1,0:T(8,128)S(1)} %get-tuple-element.12.refs_2_, bf16[256,512]{1,0:T(8,128)(2,1)S(1)} %get-tuple-element.13.refs_3_, bf16[256,128]{1,0:T(8,128)(2,1)S(1)} %get-tuple-element.14.refs_4_, ...), custom_call_target="tpu_custom_call" | custom-call | tf_op jit(solution)/shard_map/after/pallas_call | solution.py:217
  (1 shorter events, 0.0 us)
Async XLA Ops:
  0.0 0.8 %copy-start.1 = (bf16[1,1,4,16,256]{4,3,2,1,0:T(8,128)(2,1)S(1)}, bf16[1,1,4,16,256]{4,3,2,1,0:T(8,128)(2,1)}, u32[]{:S(2)}) copy-start(bf16[1,1,4,16,256]{4,3,2,1,0:T(8,128)(2,1)} %param.10) | copy-start | bytes 98308
  0.0 0.8 %copy-start = (bf16[1,1,4,16,256]{4,3,2,1,0:T(8,128)(2,1)S(1)}, bf16[1,1,4,16,256]{4,3,2,1,0:T(8,128)(2,1)}, u32[]{:S(2)}) copy-start(bf16[1,1,4,16,256]{4,3,2,1,0:T(8,128)(2,1)} %param.9) | copy-start | bytes 98308
  0.8 9.3 %collective-permute-start.3 = (bf16[2,2,16,256]{3,2,1,0:T(8,128)(2,1)S(1)}, bf16[2,2,16,256]{3,2,1,0:T(8,128)(2,1)S(1)}, u32[]{:S(2)}, u32[]{:S(2)}) collective-permute-start(bf16[2,2,16,256]{3,2,1,0:T(8,128)(2,1)S(1)} %get-tuple-element.15), channel_id=1, source_target_pairs={{0,6},{1,7},{2,8},{3,9},{4,5},{5,4},{6,14},{7,15},{8,2},{9,3},{10,... | collective-permute-start | bytes 98312 | tf_op jit(solution)/shard_map/ppermute | solution.py:193
  4.8 5.3 %collective-permute-start = (bf16[2,2,16,256]{3,2,1,0:T(8,128)(2,1)S(1)}, bf16[2,2,16,256]{3,2,1,0:T(8,128)(2,1)S(1)}, u32[]{:S(2)}, u32[]{:S(2)}) collective-permute-start(bf16[2,2,16,256]{3,2,1,0:T(8,128)(2,1)S(1)} %get-tuple-element.17), channel_id=1, source_target_pairs={{0,2},{1,3},{2,10},{3,11},{4,6},{5,7},{6,12},{7,13},{8,0},{9,1},{1... | collective-permute-start | bytes 98312 | tf_op jit(solution)/shard_map/ppermute | solution.py:193
  6.3 4.3 %collective-permute-start.1 = (bf16[2,2,16,256]{3,2,1,0:T(8,128)(2,1)S(1)}, bf16[2,2,16,256]{3,2,1,0:T(8,128)(2,1)S(1)}, u32[]{:S(2)}, u32[]{:S(2)}) collective-permute-start(bf16[2,2,16,256]{3,2,1,0:T(8,128)(2,1)S(1)} %get-tuple-element.18), channel_id=1, source_target_pairs={{0,4},{1,5},{2,12},{3,13},{4,0},{5,1},{6,10},{7,11},{8,6},{9,7},{1... | collective-permute-start | bytes 98312 | tf_op jit(solution)/shard_map/ppermute | solution.py:193
  7.9 2.7 %collective-permute-start.2 = (bf16[2,2,16,256]{3,2,1,0:T(8,128)(2,1)S(1)}, bf16[2,2,16,256]{3,2,1,0:T(8,128)(2,1)S(1)}, u32[]{:S(2)}, u32[]{:S(2)}) collective-permute-start(bf16[2,2,16,256]{3,2,1,0:T(8,128)(2,1)S(1)} %get-tuple-element.19), channel_id=1, source_target_pairs={{0,1},{1,0},{2,14},{3,15},{4,2},{5,3},{6,8},{7,9},{8,4},{9,5},{10,... | collective-permute-start | bytes 98312 | tf_op jit(solution)/shard_map/ppermute | solution.py:193

commit v6 on v5

--- a/solution.py
+++ b/solution.py
@@ -12,10 +12,10 @@
 
 TUNED = {
     (4, 2): (
-        (1, 5, 3, 6, 0, 4, 2, 7),
+        (3, 4, 2, 6, 1, 5, 0, 7),
+        (1, 5, 3, 7, 0, 4, 2, 6),
         (2, 6, 0, 5, 3, 7, 1, 4),
         (0, 7, 1, 4, 2, 6, 3, 5),
-        (3, 4, 2, 7, 1, 5, 0, 6),
     ),
 }
 
@@ -91,17 +91,51 @@
     return lax.broadcasted_iota(jnp.int32, shape, dim)
 
 
-def pick(which, taps, row):
-    out = jnp.zeros(which.shape, jnp.float32)
-    for k in range(taps.shape[1]):
-        out = jnp.where(which == k, taps[row : row + 1, k : k + 1], out)
-    return out.astype(jnp.bfloat16)
-
-
-def before(sizes, ring, owners_ref, taps_ref, words_ref, field_ref, pred_ref, valid_ref, colt_ref, rowt_ref, pick_ref, pad):
+def pack(steps, ring, scene_ref, sigma_ref, *outs):
+    n_tile, n_mem = ring
+    per = n_tile // n_mem
+    blocks, (own_ref,) = outs[:n_tile], outs[n_tile:]
+    for p in range(n_tile):
+        at = pl.ds(sent_block(n_tile, n_mem, p, steps[p]) * CAP, CAP)
+        blocks[p][0] = scene_ref[at]
+        blocks[p][1] = sigma_ref[at]
+    at = pl.ds(lax.axis_index("tile") % per * CAP, CAP)
+    own_ref[0] = scene_ref[at]
+    own_ref[1] = sigma_ref[at]
+
+
+class Band:
+    def __init__(self, taps, shape):
+        self.taps = [jnp.broadcast_to(tap, shape) for tap in taps]
+        self.shape, self.made = shape, {}
+        self.row, self.lane = iota(shape, 0), iota(shape, 1)
+
+    def tile(self, row_mul, lane_mul, offset, first=None, length=None):
+        ends = [offset + r * row_mul * (self.shape[0] - 1) + c * lane_mul * (self.shape[1] - 1) for r in (0, 1) for c in (0, 1)]
+        outside = max(ends) < 0 or min(ends) >= len(self.taps)
+        if first is not None:
+            outside = outside or first >= self.shape[1] or first + length <= 0
+        key = None if outside else (row_mul, lane_mul, offset, first)
+        if key not in self.made:
+            out = jnp.zeros(self.shape, jnp.float32)
+            if not outside:
+                which = self.row * row_mul + self.lane * lane_mul + offset
+                if first is not None:
+                    inside = jnp.logical_and(self.lane >= first, self.lane < first + length)
+                    which = jnp.where(inside, which, -1)
+                for k, tap in enumerate(self.taps):
+                    out = jnp.where(which == k, tap, out)
+            self.made[key] = out.astype(jnp.bfloat16)
+        return self.made[key]
+
+
+def before(sizes, ring, owners_ref, taps_ref, words_ref, lai_ref, pred_ref, valid_ref, colt_ref, rowt_ref, pick_ref, *scratch):
     tiles, chunk, members, rows, cols = sizes
     half_r, half_c = rows // 2, cols // 2
     n_words = words_ref.shape[1]
+    pad, col, rowd, field_ref, sem = scratch
+    fetch = pltpu.make_async_copy(lai_ref, field_ref, sem)
+    fetch.start()
     owner = [owners_ref[0, t] for t in range(tiles)]
     for t in range(tiles):
         rank = 0
@@ -113,34 +147,46 @@
     reach = taps.shape[1] // 2
     fields = chunk * members
     fr, fh = fields * rows, fields * half_r
-    i, r = iota((fh, fr), 0), iota((fh, fr), 1)
-    row_bd = jnp.where(
-        i // half_r == r // rows, r % rows - 2 * (i % half_r) + reach, -1
-    )
-    row_bd = pick(row_bd, taps, 0)
-    i, r = iota((fr, fh), 1), iota((fr, fh), 0)
-    rowt = jnp.where(i // half_r == r // rows, r % rows - 2 * (i % half_r) + reach, -1)
-    rowt_ref[...] = pick(rowt, taps, 0)
-    col = pick(iota((cols, half_c), 0) - 2 * iota((cols, half_c), 1) + reach, taps, 1)
-    colt_ref[...] = pick(iota((half_c, cols), 1) - 2 * iota((half_c, cols), 0) + reach, taps, 1)
-    for g in range(tiles // chunk):
-        field = field_ref[g * fr : (g + 1) * fr, :]
-        blurred = jnp.dot(row_bd, field, preferred_element_type=jnp.float32).astype(jnp.bfloat16)
-        pred_ref[g * fh : (g + 1) * fh, :] = jnp.dot(
-            blurred, col, preferred_element_type=jnp.float32
-        ).astype(jnp.bfloat16)
+    high, wide = 16, 128
+    down = Band([taps[0:1, k : k + 1] for k in range(taps.shape[1])], (high, wide))
+    across = Band([taps[1:2, k : k + 1] for k in range(taps.shape[1])], (high, wide))
+    for r in range(0, cols, high):
+        for c in range(0, half_c, wide):
+            col[r : r + high, c : c + wide] = across.tile(1, -2, r - 2 * c + reach)
+    for r in range(0, half_c, high):
+        for c in range(0, cols, wide):
+            colt_ref[r : r + high, c : c + wide] = across.tile(-2, 1, c - 2 * r + reach)
+    for r in range(0, fh, high):
+        top = r // half_r * rows
+        for c in range(0, fr, wide):
+            rowd[r : r + high, c : c + wide] = down.tile(-2, 1, c - top - 2 * (r % half_r) + reach, top - c, rows)
+    for r in range(0, rowt_ref.shape[0], high):
+        left = r // rows * half_r
+        width = min(wide, rowt_ref.shape[1])
+        for c in range(0, rowt_ref.shape[1], width):
+            tile = down.tile(1, -2, r % rows + 2 * (left - c) + reach, left - c, half_r)
+            rowt_ref[r : r + high, c : c + width] = tile[:, :width]
     pad[...] = jnp.zeros(pad.shape, jnp.int32)
     pad[:, :n_words] = words_ref[...]
     per_row = half_c // 2 // 32
-    for t in range(tiles):
-        words = jnp.broadcast_to(pad[t : t + 1, :], (8, 128))
-        for i0 in range(0, half_r, 8):
-            for j0 in range(0, half_c, 128):
-                i = iota((8, 128), 0) + i0
-                j = iota((8, 128), 1) + j0
-                word = jnp.take_along_axis(words, i // 2 * per_row + j // 64, axis=1)
-                bit = jnp.bitwise_and(jnp.right_shift(word, j // 2 % 32), 1)
-                valid_ref[t * half_r + i0 : t * half_r + i0 + 8, j0 : j0 + 128] = bit.astype(jnp.float32)
+    for i0 in range(0, half_r, 8):
+        for j0 in range(0, half_c, wide):
+            i = iota((8, wide), 0) + i0
+            j = iota((8, wide), 1) + j0
+            which = jnp.right_shift(i, 1) * per_row + jnp.right_shift(j, 6)
+            shift = jnp.bitwise_and(jnp.right_shift(j, 1), 31)
+            for t in range(tiles):
+                words = jnp.broadcast_to(pad[t : t + 1, :], (8, wide))
+                word = jnp.take_along_axis(words, which, axis=1)
+                bit = jnp.bitwise_and(jnp.right_shift(word, shift), 1)
+                valid_ref[t * half_r + i0 : t * half_r + i0 + 8, j0 : j0 + wide] = bit.astype(jnp.float32)
+    fetch.wait()
+    for g in range(tiles // chunk):
+        field = field_ref[g * fr : (g + 1) * fr, :]
+        blurred = jnp.dot(rowd[...], field, preferred_element_type=jnp.float32).astype(jnp.bfloat16)
+        pred_ref[g * fh : (g + 1) * fh, :] = jnp.dot(
+            blurred, col[...], preferred_element_type=jnp.float32
+        ).astype(jnp.bfloat16)
 
 
 def after(sizes, n_tile, pick_ref, pred_ref, valid_ref, colt_ref, rowt_ref, own_ref, *refs):
@@ -153,8 +199,8 @@
         for r in range(CAP):
             for kind in range(2):
                 scenes[p * CAP + r, kind] = block[kind, r]
-    cuts = PIECES if fields % PIECES == 0 else 1
-    pr, ph = fr // cuts, fh // cuts
+    pr, ph = rowt_ref.shape
+    cuts = fr // pr
     copies = []
     for g in range(tiles // chunk):
         parts = []
@@ -171,7 +217,7 @@
         for c in range(cuts):
             at = pl.ds(g * fr + c * pr, pr)
             update[at, :] = jnp.dot(
-                rowt_ref[:pr, :ph], spread[c * ph : (c + 1) * ph, :], preferred_element_type=jnp.float32
+                rowt_ref[...], spread[c * ph : (c + 1) * ph, :], preferred_element_type=jnp.float32
             ).astype(jnp.bfloat16)
             copies.append(pltpu.make_async_copy(update.at[at, :], out_ref.at[at, :], sems.at[len(copies)]))
             copies[-1].start()
@@ -183,37 +229,46 @@
     n_tile, n_mem = lax.axis_size("tile"), lax.axis_size("member")
     _, tiles, members, rows, cols = sim_lai.shape
     half_r, half_c = rows // 2, cols // 2
-    per = n_tile // n_mem
-    both = jnp.stack([scene_lai[0, 0], scene_sigma[0, 0]], 0)
-    own = lax.dynamic_slice_in_dim(both, lax.axis_index("tile") % per * CAP, CAP, 1)
-    steps = plan(n_tile, n_mem)
-    arrived = []
-    for p in range(n_tile):
-        block = lax.dynamic_slice_in_dim(both, sent_block(n_tile, n_mem, p, steps[p]) * CAP, CAP, 1)
-        arrived.append(lax.ppermute(block, GROUP, pairs(steps[p], lax.axis_size("date"))))
-    arrived = [pltpu.with_memory_space_constraint(x, pltpu.VMEM) for x in arrived]
     chunk = chunk_tiles(tiles, members, rows)
     sizes = (tiles, chunk, members, rows, cols)
     fields = chunk * members
     fr, fh = fields * rows, fields * half_r
+    cuts = PIECES if fields % PIECES == 0 else 1
     vmem = pl.BlockSpec(memory_space=pltpu.VMEM)
     smem = pl.BlockSpec(memory_space=pltpu.SMEM)
+    here = lambda x: pltpu.with_memory_space_constraint(x, pltpu.VMEM)
+    scalars = lambda x: pltpu.with_memory_space_constraint(x, pltpu.SMEM)
+    steps = plan(n_tile, n_mem)
+    block = pltpu.VMEM((2, CAP, half_r, half_c), jnp.bfloat16)
+    *blocks, own = pl.pallas_call(
+        lambda *refs: pack(steps, (n_tile, n_mem), *refs),
+        out_shape=[block] * (n_tile + 1),
+        in_specs=[vmem] * 2,
+        out_specs=[vmem] * (n_tile + 1),
+        name="pack",
+    )(scene_lai[0, 0], scene_sigma[0, 0])
+    n_date = lax.axis_size("date")
+    arrived = [here(lax.ppermute(blocks[p], GROUP, pairs(steps[p], n_date))) for p in range(n_tile)]
     pred, valid, colt, rowt, picks = pl.pallas_call(
         lambda *refs: before(sizes, (n_tile, n_mem), *refs),
         out_shape=(
             pltpu.VMEM((tiles * members * half_r, half_c), jnp.bfloat16),
             pltpu.VMEM((tiles * half_r, half_c), jnp.float32),
             pltpu.VMEM((half_c, cols), jnp.bfloat16),
-            pltpu.VMEM((fr, fh), jnp.bfloat16),
+            pltpu.VMEM((fr // cuts, fh // cuts), jnp.bfloat16),
             pltpu.SMEM((tiles,), jnp.int32),
         ),
-        in_specs=[smem] + [vmem] * 3,
+        in_specs=[smem, vmem, vmem, pl.BlockSpec(memory_space=pl.ANY)],
         out_specs=[vmem] * 4 + [smem],
-        scratch_shapes=[pltpu.VMEM((tiles, 128), jnp.int32)],
+        scratch_shapes=[
+            pltpu.VMEM((tiles, 128), jnp.int32),
+            pltpu.VMEM((cols, half_c), jnp.bfloat16),
+            pltpu.VMEM((fh, fr), jnp.bfloat16),
+            pltpu.VMEM((tiles * members * rows, cols), jnp.bfloat16),
+            pltpu.SemaphoreType.DMA,
+        ],
         name="before",
     )(owner_ids, mtf_taps, cloud_words[0], sim_lai.reshape(tiles * members * rows, cols))
-    resident = [pltpu.with_memory_space_constraint(x, pltpu.VMEM) for x in (pred, valid, colt, rowt, own)]
-    picks = pltpu.with_memory_space_constraint(picks, pltpu.SMEM)
     out = pl.pallas_call(
         lambda *refs: after(sizes, n_tile, *refs),
         out_shape=jax.ShapeDtypeStruct((tiles * members * rows, cols), jnp.bfloat16),
@@ -222,10 +277,10 @@
         scratch_shapes=[
             pltpu.VMEM(((n_tile + 1) * CAP, 2, half_r, half_c), jnp.bfloat16),
             pltpu.VMEM((tiles * members * rows, cols), jnp.bfloat16),
-            pltpu.SemaphoreType.DMA((PIECES * tiles // chunk,)),
+            pltpu.SemaphoreType.DMA((cuts * tiles // chunk,)),
         ],
         name="after",
-    )(picks, *resident, *arrived)
+    )(scalars(picks), *[here(x) for x in (pred, valid, colt, rowt, own)], *arrived)
     return out.reshape(sim_lai.shape)
 
 

time: 11.9 us -> 11.7 us (0.983)
  local copies, waits for them, and re-layouts: 0.77 us -> 0 us
  Pallas kernels: 3.2 us -> 3.88 us
  waiting for transfers between devices: 0.54 us -> 0.39 us
    pallas_call x0 -> x1, Pallas kernels: none -> 0.79 us  [per_device(): pl.pallas_call(lambda *refs: pack(steps, (n_tile, n_mem), *refs), out_sha...]
    unnamed x4 -> x0, local copies, waits for them, and re-layouts: 0.77 us -> none
    ppermute x4, waiting for transfers between devices: 0.54 us -> 0.39 us  [per_device(): lax.ppermute(blocks[p], GROUP, pairs(steps[p], n_date))]
where the time goes in v6:
time: 11.7 us; the launch traced here: 11.4 us
  starting transfers between devices  7.12 us (61%)
  Pallas kernels  3.88 us (33%)
  waiting for transfers between devices  0.39 us (3%)
    ppermute x4, starting transfers between devices, per_device(): lax.ppermute(blocks[p], GROUP, pairs(steps[p], n_date))  7.12 us
    pallas_call x1, Pallas kernels, per_device(): pl.pallas_call(lambda *refs: before(sizes, (n_tile, n_mem), *refs), out_s...  2.04 us
    pallas_call x1, Pallas kernels, per_device(): pl.pallas_call(lambda *refs: after(sizes, n_tile, *refs), out_shape=jax.S...  1.05 us
    pallas_call x1, Pallas kernels, per_device(): pl.pallas_call(lambda *refs: pack(steps, (n_tile, n_mem), *refs), out_sha...  0.79 us
    ppermute x4, waiting for transfers between devices, per_device(): lax.ppermute(blocks[p], GROUP, pairs(steps[p], n_date))  0.39 us
  transfers between devices with their start and end apart: 4, of which 1 were waited for; matrix products, arithmetic and copies ran while one was open for 0% of the time, Pallas kernels for 18%

profile of v6, /device:TPU:0, one launch (start us, length us, event | category | flops | bytes accessed | tf_op | source)
XLA Modules:
  0.0 11.4 jit_solution(17064253148355111799)
XLA Ops:
  0.0 0.8 %pack.1 = (bf16[2,2,16,256]{3,2,1,0:T(8,128)(2,1)S(1)}, bf16[2,2,16,256]{3,2,1,0:T(8,128)(2,1)S(1)}, bf16[2,2,16,256]{3,2,1,0:T(8,128)(2,1)S(1)}, bf16[2,2,16,25...) custom-call(bf16[4,16,256]{2,1,0:T(8,128)(2,1)} %bitcast.6, bf16[4,16,256]{2,1,0:T(8,128)(2,1)} %bitcast.7), custom_call_target="tpu_custom_call" | custom-call | tf_op jit(solution)/shard_map/pack/pallas_call | solution.py:243
  0.8 4.0 %collective-permute-start = (bf16[2,2,16,256]{3,2,1,0:T(8,128)(2,1)S(1)}, bf16[2,2,16,256]{3,2,1,0:T(8,128)(2,1)S(1)}, u32[]{:S(2)}, u32[]{:S(2)}) collective-permute-start(bf16[2,2,16,256]{3,2,1,0:T(8,128)(2,1)S(1)} %get-tuple-element.21), channel_id=1, source_target_pairs={{0,6},{1,7},{2,8},{3,9},{4,5},{5,4},{6,12},{7,13},{8,2},{9,3},{10,... | collective-permute-start | bytes 98312 | tf_op jit(solution)/shard_map/ppermute | solution.py:251
  4.8 1.5 %collective-permute-start.1 = (bf16[2,2,16,256]{3,2,1,0:T(8,128)(2,1)S(1)}, bf16[2,2,16,256]{3,2,1,0:T(8,128)(2,1)S(1)}, u32[]{:S(2)}, u32[]{:S(2)}) collective-permute-start(bf16[2,2,16,256]{3,2,1,0:T(8,128)(2,1)S(1)} %get-tuple-element.22), channel_id=1, source_target_pairs={{0,2},{1,3},{2,10},{3,11},{4,6},{5,7},{6,14},{7,15},{8,0},{9,1},{1... | collective-permute-start | bytes 98312 | tf_op jit(solution)/shard_map/ppermute | solution.py:251
  6.3 1.6 %collective-permute-start.2 = (bf16[2,2,16,256]{3,2,1,0:T(8,128)(2,1)S(1)}, bf16[2,2,16,256]{3,2,1,0:T(8,128)(2,1)S(1)}, u32[]{:S(2)}, u32[]{:S(2)}) collective-permute-start(bf16[2,2,16,256]{3,2,1,0:T(8,128)(2,1)S(1)} %get-tuple-element.23), channel_id=1, source_target_pairs={{0,4},{1,5},{2,12},{3,13},{4,0},{5,1},{6,10},{7,11},{8,6},{9,7},{1... | collective-permute-start | bytes 98312 | tf_op jit(solution)/shard_map/ppermute | solution.py:251
  7.9 0.0 collective-permute-start.3
  7.9 2.0 %before.1 = (bf16[128,256]{1,0:T(8,128)(2,1)S(1)}, f32[64,256]{1,0:T(8,128)S(1)}, bf16[256,512]{1,0:T(8,128)(2,1)S(1)}, bf16[128,64]{1,0:T(8,128)(2,1)S(1)}, s32[4]{0:T(128)S(4)}) custom-call(s32[1,4]{1,0:T(1,128)} %refs_0_.1, f32[2,7]{1,0:T(2,128)} %refs_1_.1, s32[4,32]{1,0:T(4,128)} %bitcast.8, bf16[256,512]{1,0:T(8,128)(2,1)} %bitcast.5), custom_call_target="tpu_custom_call" | custom-call | tf_op jit(solution)/shard_map/before/pallas_call | solution.py:252
  10.0 0.0 collective-permute-done.refs_6_
  10.0 0.0 collective-permute-done.1.refs_7_
  10.0 0.4 %collective-permute-done.2.refs_8_ = bf16[2,2,16,256]{3,2,1,0:T(8,128)(2,1)S(1)} collective-permute-done((bf16[2,2,16,256]{3,2,1,0:T(8,128)(2,1)S(1)}, bf16[2,2,16,256]{3,2,1,0:T(8,128)(2,1)S(1)}, u32[]{:S(2)}, u32[]{:S(2)}) %collective-permute-start.2) | collective-permute-done | bytes 32800 | tf_op jit(solution)/shard_map/ppermute | solution.py:251
  10.4 0.0 collective-permute-done.3.refs_9_
  10.4 1.1 %after.1 = bf16[256,512]{1,0:T(8,128)(2,1)} custom-call(s32[4]{0:T(128)S(4)} %get-tuple-element.15.refs_0_, bf16[128,256]{1,0:T(8,128)(2,1)S(1)} %get-tuple-element.16.refs_1_, f32[64,256]{1,0:T(8,128)S(1)} %get-tuple-element.17.refs_2_, bf16[256,512]{1,0:T(8,128)(2,1)S(1)} %get-tuple-element.18.refs_3_, bf16[128,64]{1,0:T(8,128)(2,1)S(1)} %get-tuple-element.19.refs_4_, ...), custom_call_target="tpu_custom_call" | custom-call | tf_op jit(solution)/shard_map/after/pallas_call | solution.py:272
Async XLA Ops:
  0.8 9.2 %collective-permute-start = (bf16[2,2,16,256]{3,2,1,0:T(8,128)(2,1)S(1)}, bf16[2,2,16,256]{3,2,1,0:T(8,128)(2,1)S(1)}, u32[]{:S(2)}, u32[]{:S(2)}) collective-permute-start(bf16[2,2,16,256]{3,2,1,0:T(8,128)(2,1)S(1)} %get-tuple-element.21), channel_id=1, source_target_pairs={{0,6},{1,7},{2,8},{3,9},{4,5},{5,4},{6,12},{7,13},{8,2},{9,3},{10,... | collective-permute-start | bytes 98312 | tf_op jit(solution)/shard_map/ppermute | solution.py:251
  4.8 5.2 %collective-permute-start.1 = (bf16[2,2,16,256]{3,2,1,0:T(8,128)(2,1)S(1)}, bf16[2,2,16,256]{3,2,1,0:T(8,128)(2,1)S(1)}, u32[]{:S(2)}, u32[]{:S(2)}) collective-permute-start(bf16[2,2,16,256]{3,2,1,0:T(8,128)(2,1)S(1)} %get-tuple-element.22), channel_id=1, source_target_pairs={{0,2},{1,3},{2,10},{3,11},{4,6},{5,7},{6,14},{7,15},{8,0},{9,1},{1... | collective-permute-start | bytes 98312 | tf_op jit(solution)/shard_map/ppermute | solution.py:251
  6.3 4.0 %collective-permute-start.2 = (bf16[2,2,16,256]{3,2,1,0:T(8,128)(2,1)S(1)}, bf16[2,2,16,256]{3,2,1,0:T(8,128)(2,1)S(1)}, u32[]{:S(2)}, u32[]{:S(2)}) collective-permute-start(bf16[2,2,16,256]{3,2,1,0:T(8,128)(2,1)S(1)} %get-tuple-element.23), channel_id=1, source_target_pairs={{0,4},{1,5},{2,12},{3,13},{4,0},{5,1},{6,10},{7,11},{8,6},{9,7},{1... | collective-permute-start | bytes 98312 | tf_op jit(solution)/shard_map/ppermute | solution.py:251
  7.9 2.5 %collective-permute-start.3 = (bf16[2,2,16,256]{3,2,1,0:T(8,128)(2,1)S(1)}, bf16[2,2,16,256]{3,2,1,0:T(8,128)(2,1)S(1)}, u32[]{:S(2)}, u32[]{:S(2)}) collective-permute-start(bf16[2,2,16,256]{3,2,1,0:T(8,128)(2,1)S(1)} %get-tuple-element.24), channel_id=1, source_target_pairs={{0,1},{1,0},{2,14},{3,15},{4,2},{5,3},{6,8},{7,9},{8,4},{9,5},{10,... | collective-permute-start | bytes 98312 | tf_op jit(solution)/shard_map/ppermute | solution.py:251

commit v7 on v6

--- a/solution.py
+++ b/solution.py
@@ -91,10 +91,10 @@
     return lax.broadcasted_iota(jnp.int32, shape, dim)
 
 
-def pack(steps, ring, scene_ref, sigma_ref, *outs):
+def pack(steps, ring, owners_ref, scene_ref, sigma_ref, taps_ref, words_ref, *outs):
     n_tile, n_mem = ring
     per = n_tile // n_mem
-    blocks, (own_ref,) = outs[:n_tile], outs[n_tile:]
+    blocks, (own_ref, taps_out, words_out, owners_out) = outs[:n_tile], outs[n_tile:]
     for p in range(n_tile):
         at = pl.ds(sent_block(n_tile, n_mem, p, steps[p]) * CAP, CAP)
         blocks[p][0] = scene_ref[at]
@@ -102,6 +102,10 @@
     at = pl.ds(lax.axis_index("tile") % per * CAP, CAP)
     own_ref[0] = scene_ref[at]
     own_ref[1] = sigma_ref[at]
+    taps_out[...] = taps_ref[...]
+    words_out[...] = words_ref[...]
+    for t in range(owners_ref.shape[1]):
+        owners_out[t] = owners_ref[0, t]
 
 
 class Band:
@@ -136,7 +140,7 @@
     pad, col, rowd, field_ref, sem = scratch
     fetch = pltpu.make_async_copy(lai_ref, field_ref, sem)
     fetch.start()
-    owner = [owners_ref[0, t] for t in range(tiles)]
+    owner = [owners_ref[t] for t in range(tiles)]
     for t in range(tiles):
         rank = 0
         for u in range(t):
@@ -240,13 +244,18 @@
     scalars = lambda x: pltpu.with_memory_space_constraint(x, pltpu.SMEM)
     steps = plan(n_tile, n_mem)
     block = pltpu.VMEM((2, CAP, half_r, half_c), jnp.bfloat16)
-    *blocks, own = pl.pallas_call(
+    *blocks, own, taps, words, owners = pl.pallas_call(
         lambda *refs: pack(steps, (n_tile, n_mem), *refs),
-        out_shape=[block] * (n_tile + 1),
-        in_specs=[vmem] * 2,
-        out_specs=[vmem] * (n_tile + 1),
+        out_shape=(
+            *[block] * (n_tile + 1),
+            pltpu.VMEM(mtf_taps.shape, jnp.float32),
+            pltpu.VMEM(cloud_words.shape[1:], jnp.int32),
+            pltpu.SMEM((tiles,), jnp.int32),
+        ),
+        in_specs=[smem] + [vmem] * 4,
+        out_specs=[vmem] * (n_tile + 3) + [smem],
         name="pack",
-    )(scene_lai[0, 0], scene_sigma[0, 0])
+    )(owner_ids, scene_lai[0, 0], scene_sigma[0, 0], mtf_taps, cloud_words[0])
     n_date = lax.axis_size("date")
     arrived = [here(lax.ppermute(blocks[p], GROUP, pairs(steps[p], n_date))) for p in range(n_tile)]
     pred, valid, colt, rowt, picks = pl.pallas_call(
@@ -268,7 +277,7 @@
             pltpu.SemaphoreType.DMA,
         ],
         name="before",
-    )(owner_ids, mtf_taps, cloud_words[0], sim_lai.reshape(tiles * members * rows, cols))
+    )(scalars(owners), here(taps), here(words), sim_lai.reshape(tiles * members * rows, cols))
     out = pl.pallas_call(
         lambda *refs: after(sizes, n_tile, *refs),
         out_shape=jax.ShapeDtypeStruct((tiles * members * rows, cols), jnp.bfloat16),

time: 11.7 us -> 11.7 us (level)
  waiting for transfers between devices: 0.39 us -> 0.96 us
  Pallas kernels: 3.88 us -> 3.36 us
    ppermute x4, waiting for transfers between devices: 0.39 us -> 0.96 us  [per_device(): lax.ppermute(blocks[p], GROUP, pairs(steps[p], n_date))]
    pallas_call x1, Pallas kernels: 2.04 us -> 1.48 us  [per_device(): pl.pallas_call(lambda *refs: before(sizes, (n_tile, n_mem), *refs), out_s...]
  transfers between devices with their start and end apart: 4 -> 4, of which waited for: 1 -> 2; matrix products, arithmetic and copies ran while one was open for 0% -> 0% of each run, Pallas kernels for 18% -> 13%
where the time goes in v7:
time: 11.7 us; the launch traced here: 11.5 us
  starting transfers between devices  7.12 us (61%)
  Pallas kernels  3.36 us (29%)
  waiting for transfers between devices  0.96 us (8%)
    ppermute x4, starting transfers between devices, per_device(): lax.ppermute(blocks[p], GROUP, pairs(steps[p], n_date))  7.12 us
    pallas_call x1, Pallas kernels, per_device(): pl.pallas_call(lambda *refs: before(sizes, (n_tile, n_mem), *refs), out_s...  1.48 us
    pallas_call x1, Pallas kernels, per_device(): pl.pallas_call(lambda *refs: after(sizes, n_tile, *refs), out_shape=jax.S...  1.05 us
    ppermute x4, waiting for transfers between devices, per_device(): lax.ppermute(blocks[p], GROUP, pairs(steps[p], n_date))  0.96 us
    pallas_call x1, Pallas kernels, per_device(): pl.pallas_call(lambda *refs: pack(steps, (n_tile, n_mem), *refs), out_sha...  0.83 us
  transfers between devices with their start and end apart: 4, of which 2 were waited for; matrix products, arithmetic and copies ran while one was open for 0% of the time, Pallas kernels for 13%

profile of v7, /device:TPU:0, one launch (start us, length us, event | category | flops | bytes accessed | tf_op | source)
XLA Modules:
  0.0 11.5 jit_solution(7920986110546092392)
XLA Ops:
  0.0 0.8 %pack.1 = (bf16[2,2,16,256]{3,2,1,0:T(8,128)(2,1)S(1)}, bf16[2,2,16,256]{3,2,1,0:T(8,128)(2,1)S(1)}, bf16[2,2,16,256]{3,2,1,0:T(8,128)(2,1)S(1)}, bf16[2,2,16,25...) custom-call(s32[1,4]{1,0:T(1,128)} %refs_0_.1, ...), custom_call_target="tpu_custom_call" | custom-call | tf_op jit(solution)/shard_map/pack/pallas_call | solution.py:247
  0.8 4.0 %collective-permute-start = (bf16[2,2,16,256]{3,2,1,0:T(8,128)(2,1)S(1)}, bf16[2,2,16,256]{3,2,1,0:T(8,128)(2,1)S(1)}, u32[]{:S(2)}, u32[]{:S(2)}) collective-permute-start(bf16[2,2,16,256]{3,2,1,0:T(8,128)(2,1)S(1)} %get-tuple-element.27), channel_id=1, source_target_pairs={{0,6},{1,7},{2,8},{3,9},{4,5},{5,4},{6,12},{7,13},{8,2},{9,3},{10,... | collective-permute-start | bytes 98312 | tf_op jit(solution)/shard_map/ppermute | solution.py:260
  4.8 1.5 %collective-permute-start.1 = (bf16[2,2,16,256]{3,2,1,0:T(8,128)(2,1)S(1)}, bf16[2,2,16,256]{3,2,1,0:T(8,128)(2,1)S(1)}, u32[]{:S(2)}, u32[]{:S(2)}) collective-permute-start(bf16[2,2,16,256]{3,2,1,0:T(8,128)(2,1)S(1)} %get-tuple-element.28), channel_id=1, source_target_pairs={{0,2},{1,3},{2,10},{3,11},{4,6},{5,7},{6,14},{7,15},{8,0},{9,1},{1... | collective-permute-start | bytes 98312 | tf_op jit(solution)/shard_map/ppermute | solution.py:260
  6.4 1.6 %collective-permute-start.2 = (bf16[2,2,16,256]{3,2,1,0:T(8,128)(2,1)S(1)}, bf16[2,2,16,256]{3,2,1,0:T(8,128)(2,1)S(1)}, u32[]{:S(2)}, u32[]{:S(2)}) collective-permute-start(bf16[2,2,16,256]{3,2,1,0:T(8,128)(2,1)S(1)} %get-tuple-element.29), channel_id=1, source_target_pairs={{0,4},{1,5},{2,12},{3,13},{4,0},{5,1},{6,10},{7,11},{8,6},{9,7},{1... | collective-permute-start | bytes 98312 | tf_op jit(solution)/shard_map/ppermute | solution.py:260
  8.0 0.0 collective-permute-start.3
  8.0 1.5 %before.1 = (bf16[128,256]{1,0:T(8,128)(2,1)S(1)}, f32[64,256]{1,0:T(8,128)S(1)}, bf16[256,512]{1,0:T(8,128)(2,1)S(1)}, bf16[128,64]{1,0:T(8,128)(2,1)S(1)}, s32[4]{0:T(128)S(4)}) custom-call(s32[4]{0:T(128)S(4)} %get-tuple-element.18.refs_0_, f32[2,7]{1,0:T(2,128)S(1)} %get-tuple-element.19.refs_1_, s32[4,32]{1,0:T(4,128)S(1)} %get-tuple-element.20.refs_2_, ...), custom_call_target="tpu_custom_call" | custom-call | tf_op jit(solution)/shard_map/before/pallas_call | solution.py:261
  9.5 0.0 collective-permute-done.refs_6_
  9.5 0.2 %collective-permute-done.1.refs_7_ = bf16[2,2,16,256]{3,2,1,0:T(8,128)(2,1)S(1)} collective-permute-done((bf16[2,2,16,256]{3,2,1,0:T(8,128)(2,1)S(1)}, bf16[2,2,16,256]{3,2,1,0:T(8,128)(2,1)S(1)}, u32[]{:S(2)}, u32[]{:S(2)}) %collective-permute-start.1) | collective-permute-done | bytes 32800 | tf_op jit(solution)/shard_map/ppermute | solution.py:260
  9.7 0.8 %collective-permute-done.2.refs_8_ = bf16[2,2,16,256]{3,2,1,0:T(8,128)(2,1)S(1)} collective-permute-done((bf16[2,2,16,256]{3,2,1,0:T(8,128)(2,1)S(1)}, bf16[2,2,16,256]{3,2,1,0:T(8,128)(2,1)S(1)}, u32[]{:S(2)}, u32[]{:S(2)}) %collective-permute-start.2) | collective-permute-done | bytes 32800 | tf_op jit(solution)/shard_map/ppermute | solution.py:260
  10.4 0.0 collective-permute-done.3.refs_9_
  10.4 1.1 %after.1 = bf16[256,512]{1,0:T(8,128)(2,1)} custom-call(s32[4]{0:T(128)S(4)} %get-tuple-element.21.refs_0_, bf16[128,256]{1,0:T(8,128)(2,1)S(1)} %get-tuple-element.22.refs_1_, f32[64,256]{1,0:T(8,128)S(1)} %get-tuple-element.23.refs_2_, bf16[256,512]{1,0:T(8,128)(2,1)S(1)} %get-tuple-element.24.refs_3_, bf16[128,64]{1,0:T(8,128)(2,1)S(1)} %get-tuple-element.25.refs_4_, ...), custom_call_target="tpu_custom_call" | custom-call | tf_op jit(solution)/shard_map/after/pallas_call | solution.py:281
Async XLA Ops:
  0.8 8.6 %collective-permute-start = (bf16[2,2,16,256]{3,2,1,0:T(8,128)(2,1)S(1)}, bf16[2,2,16,256]{3,2,1,0:T(8,128)(2,1)S(1)}, u32[]{:S(2)}, u32[]{:S(2)}) collective-permute-start(bf16[2,2,16,256]{3,2,1,0:T(8,128)(2,1)S(1)} %get-tuple-element.27), channel_id=1, source_target_pairs={{0,6},{1,7},{2,8},{3,9},{4,5},{5,4},{6,12},{7,13},{8,2},{9,3},{10,... | collective-permute-start | bytes 98312 | tf_op jit(solution)/shard_map/ppermute | solution.py:260
  4.8 4.8 %collective-permute-start.1 = (bf16[2,2,16,256]{3,2,1,0:T(8,128)(2,1)S(1)}, bf16[2,2,16,256]{3,2,1,0:T(8,128)(2,1)S(1)}, u32[]{:S(2)}, u32[]{:S(2)}) collective-permute-start(bf16[2,2,16,256]{3,2,1,0:T(8,128)(2,1)S(1)} %get-tuple-element.28), channel_id=1, source_target_pairs={{0,2},{1,3},{2,10},{3,11},{4,6},{5,7},{6,14},{7,15},{8,0},{9,1},{1... | collective-permute-start | bytes 98312 | tf_op jit(solution)/shard_map/ppermute | solution.py:260
  6.4 4.0 %collective-permute-start.2 = (bf16[2,2,16,256]{3,2,1,0:T(8,128)(2,1)S(1)}, bf16[2,2,16,256]{3,2,1,0:T(8,128)(2,1)S(1)}, u32[]{:S(2)}, u32[]{:S(2)}) collective-permute-start(bf16[2,2,16,256]{3,2,1,0:T(8,128)(2,1)S(1)} %get-tuple-element.29), channel_id=1, source_target_pairs={{0,4},{1,5},{2,12},{3,13},{4,0},{5,1},{6,10},{7,11},{8,6},{9,7},{1... | collective-permute-start | bytes 98312 | tf_op jit(solution)/shard_map/ppermute | solution.py:260
  8.0 2.5 %collective-permute-start.3 = (bf16[2,2,16,256]{3,2,1,0:T(8,128)(2,1)S(1)}, bf16[2,2,16,256]{3,2,1,0:T(8,128)(2,1)S(1)}, u32[]{:S(2)}, u32[]{:S(2)}) collective-permute-start(bf16[2,2,16,256]{3,2,1,0:T(8,128)(2,1)S(1)} %get-tuple-element.30), channel_id=1, source_target_pairs={{0,1},{1,0},{2,14},{3,15},{4,2},{5,3},{6,8},{7,9},{8,4},{9,5},{10,... | collective-permute-start | bytes 98312 | tf_op jit(solution)/shard_map/ppermute | solution.py:260

commit v8 on v6

--- a/solution.py
+++ b/solution.py
@@ -6,7 +6,7 @@
 from jax.sharding import PartitionSpec as P
 
 CAP = 2
-PIECES = 2
+PIECES = 4
 GROUP = ("tile", "member", "date")
 
 

time: 11.7 us -> 11.6 us (level)
  no operation moved by 1% of the time
where the time goes in v8:
time: 11.6 us; the launch traced here: 11.4 us
  starting transfers between devices  7.12 us (61%)
  Pallas kernels  3.91 us (34%)
  waiting for transfers between devices  0.34 us (3%)
    ppermute x4, starting transfers between devices, per_device(): lax.ppermute(blocks[p], GROUP, pairs(steps[p], n_date))  7.12 us
    pallas_call x1, Pallas kernels, per_device(): pl.pallas_call(lambda *refs: before(sizes, (n_tile, n_mem), *refs), out_s...  2.09 us
    pallas_call x1, Pallas kernels, per_device(): pl.pallas_call(lambda *refs: after(sizes, n_tile, *refs), out_shape=jax.S...  1.03 us
    pallas_call x1, Pallas kernels, per_device(): pl.pallas_call(lambda *refs: pack(steps, (n_tile, n_mem), *refs), out_sha...  0.79 us
    ppermute x4, waiting for transfers between devices, per_device(): lax.ppermute(blocks[p], GROUP, pairs(steps[p], n_date))  0.34 us
  transfers between devices with their start and end apart: 4, of which 1 were waited for; matrix products, arithmetic and copies ran while one was open for 0% of the time, Pallas kernels for 18%

profile of v8, /device:TPU:0, one launch (start us, length us, event | category | flops | bytes accessed | tf_op | source)
XLA Modules:
  0.0 11.4 jit_solution(2582542414486404734)
XLA Ops:
  0.0 0.8 %pack.1 = (bf16[2,2,16,256]{3,2,1,0:T(8,128)(2,1)S(1)}, bf16[2,2,16,256]{3,2,1,0:T(8,128)(2,1)S(1)}, bf16[2,2,16,256]{3,2,1,0:T(8,128)(2,1)S(1)}, bf16[2,2,16,25...) custom-call(bf16[4,16,256]{2,1,0:T(8,128)(2,1)} %bitcast.6, bf16[4,16,256]{2,1,0:T(8,128)(2,1)} %bitcast.7), custom_call_target="tpu_custom_call" | custom-call | tf_op jit(solution)/shard_map/pack/pallas_call | solution.py:243
  0.8 4.0 %collective-permute-start = (bf16[2,2,16,256]{3,2,1,0:T(8,128)(2,1)S(1)}, bf16[2,2,16,256]{3,2,1,0:T(8,128)(2,1)S(1)}, u32[]{:S(2)}, u32[]{:S(2)}) collective-permute-start(bf16[2,2,16,256]{3,2,1,0:T(8,128)(2,1)S(1)} %get-tuple-element.21), channel_id=1, source_target_pairs={{0,6},{1,7},{2,8},{3,9},{4,5},{5,4},{6,12},{7,13},{8,2},{9,3},{10,... | collective-permute-start | bytes 98312 | tf_op jit(solution)/shard_map/ppermute | solution.py:251
  4.8 1.5 %collective-permute-start.1 = (bf16[2,2,16,256]{3,2,1,0:T(8,128)(2,1)S(1)}, bf16[2,2,16,256]{3,2,1,0:T(8,128)(2,1)S(1)}, u32[]{:S(2)}, u32[]{:S(2)}) collective-permute-start(bf16[2,2,16,256]{3,2,1,0:T(8,128)(2,1)S(1)} %get-tuple-element.22), channel_id=1, source_target_pairs={{0,2},{1,3},{2,10},{3,11},{4,6},{5,7},{6,14},{7,15},{8,0},{9,1},{1... | collective-permute-start | bytes 98312 | tf_op jit(solution)/shard_map/ppermute | solution.py:251
  6.3 1.6 %collective-permute-start.2 = (bf16[2,2,16,256]{3,2,1,0:T(8,128)(2,1)S(1)}, bf16[2,2,16,256]{3,2,1,0:T(8,128)(2,1)S(1)}, u32[]{:S(2)}, u32[]{:S(2)}) collective-permute-start(bf16[2,2,16,256]{3,2,1,0:T(8,128)(2,1)S(1)} %get-tuple-element.23), channel_id=1, source_target_pairs={{0,4},{1,5},{2,12},{3,13},{4,0},{5,1},{6,10},{7,11},{8,6},{9,7},{1... | collective-permute-start | bytes 98312 | tf_op jit(solution)/shard_map/ppermute | solution.py:251
  7.9 0.0 collective-permute-start.3
  7.9 2.1 %before.1 = (bf16[128,256]{1,0:T(8,128)(2,1)S(1)}, f32[64,256]{1,0:T(8,128)S(1)}, bf16[256,512]{1,0:T(8,128)(2,1)S(1)}, bf16[64,32]{1,0:T(8,128)(2,1)S(1)}, s32[4]{0:T(128)S(4)}) custom-call(s32[1,4]{1,0:T(1,128)} %refs_0_.1, f32[2,7]{1,0:T(2,128)} %refs_1_.1, s32[4,32]{1,0:T(4,128)} %bitcast.8, bf16[256,512]{1,0:T(8,128)(2,1)} %bitcast.5), custom_call_target="tpu_custom_call" | custom-call | tf_op jit(solution)/shard_map/before/pallas_call | solution.py:252
  10.0 0.0 collective-permute-done.refs_6_
  10.0 0.0 collective-permute-done.1.refs_7_
  10.0 0.3 %collective-permute-done.2.refs_8_ = bf16[2,2,16,256]{3,2,1,0:T(8,128)(2,1)S(1)} collective-permute-done((bf16[2,2,16,256]{3,2,1,0:T(8,128)(2,1)S(1)}, bf16[2,2,16,256]{3,2,1,0:T(8,128)(2,1)S(1)}, u32[]{:S(2)}, u32[]{:S(2)}) %collective-permute-start.2) | collective-permute-done | bytes 32800 | tf_op jit(solution)/shard_map/ppermute | solution.py:251
  10.4 0.0 collective-permute-done.3.refs_9_
  10.4 1.0 %after.1 = bf16[256,512]{1,0:T(8,128)(2,1)} custom-call(s32[4]{0:T(128)S(4)} %get-tuple-element.15.refs_0_, bf16[128,256]{1,0:T(8,128)(2,1)S(1)} %get-tuple-element.16.refs_1_, f32[64,256]{1,0:T(8,128)S(1)} %get-tuple-element.17.refs_2_, bf16[256,512]{1,0:T(8,128)(2,1)S(1)} %get-tuple-element.18.refs_3_, bf16[64,32]{1,0:T(8,128)(2,1)S(1)} %get-tuple-element.19.refs_4_, ...), custom_call_target="tpu_custom_call" | custom-call | tf_op jit(solution)/shard_map/after/pallas_call | solution.py:272
Async XLA Ops:
  0.8 9.2 %collective-permute-start = (bf16[2,2,16,256]{3,2,1,0:T(8,128)(2,1)S(1)}, bf16[2,2,16,256]{3,2,1,0:T(8,128)(2,1)S(1)}, u32[]{:S(2)}, u32[]{:S(2)}) collective-permute-start(bf16[2,2,16,256]{3,2,1,0:T(8,128)(2,1)S(1)} %get-tuple-element.21), channel_id=1, source_target_pairs={{0,6},{1,7},{2,8},{3,9},{4,5},{5,4},{6,12},{7,13},{8,2},{9,3},{10,... | collective-permute-start | bytes 98312 | tf_op jit(solution)/shard_map/ppermute | solution.py:251
  4.8 5.2 %collective-permute-start.1 = (bf16[2,2,16,256]{3,2,1,0:T(8,128)(2,1)S(1)}, bf16[2,2,16,256]{3,2,1,0:T(8,128)(2,1)S(1)}, u32[]{:S(2)}, u32[]{:S(2)}) collective-permute-start(bf16[2,2,16,256]{3,2,1,0:T(8,128)(2,1)S(1)} %get-tuple-element.22), channel_id=1, source_target_pairs={{0,2},{1,3},{2,10},{3,11},{4,6},{5,7},{6,14},{7,15},{8,0},{9,1},{1... | collective-permute-start | bytes 98312 | tf_op jit(solution)/shard_map/ppermute | solution.py:251
  6.3 4.0 %collective-permute-start.2 = (bf16[2,2,16,256]{3,2,1,0:T(8,128)(2,1)S(1)}, bf16[2,2,16,256]{3,2,1,0:T(8,128)(2,1)S(1)}, u32[]{:S(2)}, u32[]{:S(2)}) collective-permute-start(bf16[2,2,16,256]{3,2,1,0:T(8,128)(2,1)S(1)} %get-tuple-element.23), channel_id=1, source_target_pairs={{0,4},{1,5},{2,12},{3,13},{4,0},{5,1},{6,10},{7,11},{8,6},{9,7},{1... | collective-permute-start | bytes 98312 | tf_op jit(solution)/shard_map/ppermute | solution.py:251
  7.9 2.5 %collective-permute-start.3 = (bf16[2,2,16,256]{3,2,1,0:T(8,128)(2,1)S(1)}, bf16[2,2,16,256]{3,2,1,0:T(8,128)(2,1)S(1)}, u32[]{:S(2)}, u32[]{:S(2)}) collective-permute-start(bf16[2,2,16,256]{3,2,1,0:T(8,128)(2,1)S(1)} %get-tuple-element.24), channel_id=1, source_target_pairs={{0,1},{1,0},{2,14},{3,15},{4,2},{5,3},{6,8},{7,9},{8,4},{9,5},{10,... | collective-permute-start | bytes 98312 | tf_op jit(solution)/shard_map/ppermute | solution.py:251

commit v9 on v7

--- a/solution.py
+++ b/solution.py
@@ -6,7 +6,7 @@
 from jax.sharding import PartitionSpec as P
 
 CAP = 2
-PIECES = 2
+PIECES = 4
 GROUP = ("tile", "member", "date")
 
 

time: 11.7 us -> 11.7 us (level)
  transfers between devices with their start and end apart: 4 -> 4, of which waited for: 2 -> 2; matrix products, arithmetic and copies ran while one was open for 0% -> 0% of each run, Pallas kernels for 13% -> 12%
where the time goes in v9:
time: 11.7 us; the launch traced here: 11.5 us
  starting transfers between devices  7.12 us (61%)
  Pallas kernels  3.26 us (28%)
  waiting for transfers between devices  1.04 us (9%)
    ppermute x4, starting transfers between devices, per_device(): lax.ppermute(blocks[p], GROUP, pairs(steps[p], n_date))  7.12 us
    pallas_call x1, Pallas kernels, per_device(): pl.pallas_call(lambda *refs: before(sizes, (n_tile, n_mem), *refs), out_s...  1.4 us
    ppermute x4, waiting for transfers between devices, per_device(): lax.ppermute(blocks[p], GROUP, pairs(steps[p], n_date))  1.04 us
    pallas_call x1, Pallas kernels, per_device(): pl.pallas_call(lambda *refs: after(sizes, n_tile, *refs), out_shape=jax.S...  1.04 us
    pallas_call x1, Pallas kernels, per_device(): pl.pallas_call(lambda *refs: pack(steps, (n_tile, n_mem), *refs), out_sha...  0.83 us
  transfers between devices with their start and end apart: 4, of which 2 were waited for; matrix products, arithmetic and copies ran while one was open for 0% of the time, Pallas kernels for 12%

profile of v9, /device:TPU:0, one launch (start us, length us, event | category | flops | bytes accessed | tf_op | source)
XLA Modules:
  0.0 11.5 jit_solution(4778540935022869488)
XLA Ops:
  0.0 0.8 %pack.1 = (bf16[2,2,16,256]{3,2,1,0:T(8,128)(2,1)S(1)}, bf16[2,2,16,256]{3,2,1,0:T(8,128)(2,1)S(1)}, bf16[2,2,16,256]{3,2,1,0:T(8,128)(2,1)S(1)}, bf16[2,2,16,25...) custom-call(s32[1,4]{1,0:T(1,128)} %refs_0_.1, ...), custom_call_target="tpu_custom_call" | custom-call | tf_op jit(solution)/shard_map/pack/pallas_call | solution.py:247
  0.8 4.0 %collective-permute-start = (bf16[2,2,16,256]{3,2,1,0:T(8,128)(2,1)S(1)}, bf16[2,2,16,256]{3,2,1,0:T(8,128)(2,1)S(1)}, u32[]{:S(2)}, u32[]{:S(2)}) collective-permute-start(bf16[2,2,16,256]{3,2,1,0:T(8,128)(2,1)S(1)} %get-tuple-element.27), channel_id=1, source_target_pairs={{0,6},{1,7},{2,8},{3,9},{4,5},{5,4},{6,12},{7,13},{8,2},{9,3},{10,... | collective-permute-start | bytes 98312 | tf_op jit(solution)/shard_map/ppermute | solution.py:260
  4.8 1.5 %collective-permute-start.1 = (bf16[2,2,16,256]{3,2,1,0:T(8,128)(2,1)S(1)}, bf16[2,2,16,256]{3,2,1,0:T(8,128)(2,1)S(1)}, u32[]{:S(2)}, u32[]{:S(2)}) collective-permute-start(bf16[2,2,16,256]{3,2,1,0:T(8,128)(2,1)S(1)} %get-tuple-element.28), channel_id=1, source_target_pairs={{0,2},{1,3},{2,10},{3,11},{4,6},{5,7},{6,14},{7,15},{8,0},{9,1},{1... | collective-permute-start | bytes 98312 | tf_op jit(solution)/shard_map/ppermute | solution.py:260
  6.4 1.6 %collective-permute-start.2 = (bf16[2,2,16,256]{3,2,1,0:T(8,128)(2,1)S(1)}, bf16[2,2,16,256]{3,2,1,0:T(8,128)(2,1)S(1)}, u32[]{:S(2)}, u32[]{:S(2)}) collective-permute-start(bf16[2,2,16,256]{3,2,1,0:T(8,128)(2,1)S(1)} %get-tuple-element.29), channel_id=1, source_target_pairs={{0,4},{1,5},{2,12},{3,13},{4,0},{5,1},{6,10},{7,11},{8,6},{9,7},{1... | collective-permute-start | bytes 98312 | tf_op jit(solution)/shard_map/ppermute | solution.py:260
  8.0 0.0 collective-permute-start.3
  8.0 1.4 %before.1 = (bf16[128,256]{1,0:T(8,128)(2,1)S(1)}, f32[64,256]{1,0:T(8,128)S(1)}, bf16[256,512]{1,0:T(8,128)(2,1)S(1)}, bf16[64,32]{1,0:T(8,128)(2,1)S(1)}, s32[4]{0:T(128)S(4)}) custom-call(s32[4]{0:T(128)S(4)} %get-tuple-element.18.refs_0_, f32[2,7]{1,0:T(2,128)S(1)} %get-tuple-element.19.refs_1_, s32[4,32]{1,0:T(4,128)S(1)} %get-tuple-element.20.refs_2_, ...), custom_call_target="tpu_custom_call" | custom-call | tf_op jit(solution)/shard_map/before/pallas_call | solution.py:261
  9.4 0.0 collective-permute-done.refs_6_
  9.4 0.3 %collective-permute-done.1.refs_7_ = bf16[2,2,16,256]{3,2,1,0:T(8,128)(2,1)S(1)} collective-permute-done((bf16[2,2,16,256]{3,2,1,0:T(8,128)(2,1)S(1)}, bf16[2,2,16,256]{3,2,1,0:T(8,128)(2,1)S(1)}, u32[]{:S(2)}, u32[]{:S(2)}) %collective-permute-start.1) | collective-permute-done | bytes 32800 | tf_op jit(solution)/shard_map/ppermute | solution.py:260
  9.7 0.8 %collective-permute-done.2.refs_8_ = bf16[2,2,16,256]{3,2,1,0:T(8,128)(2,1)S(1)} collective-permute-done((bf16[2,2,16,256]{3,2,1,0:T(8,128)(2,1)S(1)}, bf16[2,2,16,256]{3,2,1,0:T(8,128)(2,1)S(1)}, u32[]{:S(2)}, u32[]{:S(2)}) %collective-permute-start.2) | collective-permute-done | bytes 32800 | tf_op jit(solution)/shard_map/ppermute | solution.py:260
  10.4 0.0 collective-permute-done.3.refs_9_
  10.4 1.0 %after.1 = bf16[256,512]{1,0:T(8,128)(2,1)} custom-call(s32[4]{0:T(128)S(4)} %get-tuple-element.21.refs_0_, bf16[128,256]{1,0:T(8,128)(2,1)S(1)} %get-tuple-element.22.refs_1_, f32[64,256]{1,0:T(8,128)S(1)} %get-tuple-element.23.refs_2_, bf16[256,512]{1,0:T(8,128)(2,1)S(1)} %get-tuple-element.24.refs_3_, bf16[64,32]{1,0:T(8,128)(2,1)S(1)} %get-tuple-element.25.refs_4_, ...), custom_call_target="tpu_custom_call" | custom-call | tf_op jit(solution)/shard_map/after/pallas_call | solution.py:281
Async XLA Ops:
  0.8 8.5 %collective-permute-start = (bf16[2,2,16,256]{3,2,1,0:T(8,128)(2,1)S(1)}, bf16[2,2,16,256]{3,2,1,0:T(8,128)(2,1)S(1)}, u32[]{:S(2)}, u32[]{:S(2)}) collective-permute-start(bf16[2,2,16,256]{3,2,1,0:T(8,128)(2,1)S(1)} %get-tuple-element.27), channel_id=1, source_target_pairs={{0,6},{1,7},{2,8},{3,9},{4,5},{5,4},{6,12},{7,13},{8,2},{9,3},{10,... | collective-permute-start | bytes 98312 | tf_op jit(solution)/shard_map/ppermute | solution.py:260
  4.8 4.8 %collective-permute-start.1 = (bf16[2,2,16,256]{3,2,1,0:T(8,128)(2,1)S(1)}, bf16[2,2,16,256]{3,2,1,0:T(8,128)(2,1)S(1)}, u32[]{:S(2)}, u32[]{:S(2)}) collective-permute-start(bf16[2,2,16,256]{3,2,1,0:T(8,128)(2,1)S(1)} %get-tuple-element.28), channel_id=1, source_target_pairs={{0,2},{1,3},{2,10},{3,11},{4,6},{5,7},{6,14},{7,15},{8,0},{9,1},{1... | collective-permute-start | bytes 98312 | tf_op jit(solution)/shard_map/ppermute | solution.py:260
  6.4 4.0 %collective-permute-start.2 = (bf16[2,2,16,256]{3,2,1,0:T(8,128)(2,1)S(1)}, bf16[2,2,16,256]{3,2,1,0:T(8,128)(2,1)S(1)}, u32[]{:S(2)}, u32[]{:S(2)}) collective-permute-start(bf16[2,2,16,256]{3,2,1,0:T(8,128)(2,1)S(1)} %get-tuple-element.29), channel_id=1, source_target_pairs={{0,4},{1,5},{2,12},{3,13},{4,0},{5,1},{6,10},{7,11},{8,6},{9,7},{1... | collective-permute-start | bytes 98312 | tf_op jit(solution)/shard_map/ppermute | solution.py:260
  8.0 2.5 %collective-permute-start.3 = (bf16[2,2,16,256]{3,2,1,0:T(8,128)(2,1)S(1)}, bf16[2,2,16,256]{3,2,1,0:T(8,128)(2,1)S(1)}, u32[]{:S(2)}, u32[]{:S(2)}) collective-permute-start(bf16[2,2,16,256]{3,2,1,0:T(8,128)(2,1)S(1)} %get-tuple-element.30), channel_id=1, source_target_pairs={{0,1},{1,0},{2,14},{3,15},{4,2},{5,3},{6,8},{7,9},{8,4},{9,5},{10,... | collective-permute-start | bytes 98312 | tf_op jit(solution)/shard_map/ppermute | solution.py:260
